TPU v7x, 256 devices: a whole 4x4x8 slice. The times are simulated.
256 devices in a mesh: feat: 4 (over y), node: 64 (over x, z, core).
Axes of the slice: x: 4, y: 4, z: 8, core: 2. Of those that a mesh axis runs over, the one named last changes fastest.
Arguments:
- features: bfloat16 [64, 768, 2048], P('node', 'feat'), may hold values from -6 to 6
- tiles: bfloat16 [64, 48, 128, 128], P('node'), may hold values from -0.3125 to 0.3125
- tile_rows: int32 [64, 48], P('node'), may hold values from 0 to 15, as said below
- tile_cols: int32 [64, 48], P('node'), may hold values from 0 to 31
- send_rows: int32 [64, 64, 32], P('node'), may hold values from 0 to 2047, as said below
- send_count: int32 [64, 64], P('node'), may hold values from 0 to 32, as said below
- w_neigh: bfloat16 [768, 1024], P('feat'), may hold values from -0.15625 to 0.15625
- w_self: bfloat16 [768, 1024], P('feat'), may hold values from -0.15625 to 0.15625
- cotangent: bfloat16 [64, 2048, 1024], P('node', 'feat'), may hold values from -16 to 16
Outputs:
- hidden: bfloat16 [64, 2048, 1024], P('node', 'feat')
- grad_features: bfloat16 [64, 768, 2048], P('node', 'feat')
- grad_neigh: float32 [768, 1024], P('feat')
- grad_self: float32 [768, 1024], P('feat')
Inputs may be any that keep to these rules, and one draw needn't show every extreme that they name: `tile_rows`: for each partition the first 16 tiles feed the row blocks 0, 1, 2 and so on in order, so that every block of rows has a tile. `send_rows`: rows may repeat within a list. `send_count`: A partition sends nothing to itself, and every partition fills all 32 slots toward at least one other partition.
All inputs are finite; a program needn't handle non-finite values.
Results may differ from a plain program's by a relative error of at most 0.0058.
Values may be sent and summed in bfloat16 or wider, within the bound.
A program may use at most 128 MiB of HBM per device.

v0:
```python
import jax
import jax.numpy as jnp
from jax import lax
from jax.sharding import PartitionSpec as P


def per_device(
    features, tiles, tile_rows, tile_cols, send_rows, send_count, w_neigh, w_self, cotangent
):
    own_cols = features[0]
    feat_dev, own_rows = own_cols.shape
    tile_vals = tiles[0]
    tile_side = tile_vals.shape[1]
    row_ids = tile_rows[0]
    col_ids = tile_cols[0]
    targets = send_rows[0]
    amounts = send_count[0]
    parts, slots = targets.shape
    live_slots = lax.broadcasted_iota(jnp.int32, (parts, slots), 1) < amounts[:, None]
    picked = jnp.take(own_cols, targets.reshape(-1), axis=1).reshape(feat_dev, parts, slots)
    picked = jnp.where(live_slots[None], picked, jnp.zeros((), own_cols.dtype))
    arrived = lax.all_to_all(picked, "node", split_axis=1, concat_axis=1, tiled=True)
    extended = jnp.concatenate([own_cols, arrived.reshape(feat_dev, parts * slots)], axis=1)
    col_blocks = extended.shape[1] // tile_side
    row_blocks = own_rows // tile_side
    gathered_cols = extended.reshape(feat_dev, col_blocks, tile_side)[:, col_ids, :]
    partial_sums = jnp.einsum(
        "fkj,kij->fki", gathered_cols, tile_vals, preferred_element_type=jnp.float32
    )
    row_onehot = (row_ids[:, None] == lax.broadcasted_iota(jnp.int32, (1, row_blocks), 1)).astype(
        jnp.float32
    )
    aggregated = jnp.einsum(
        "fki,kr->fri", partial_sums, row_onehot, precision=lax.Precision.HIGHEST
    )
    aggregated = aggregated.reshape(feat_dev, own_rows).astype(jnp.bfloat16)
    full_neigh, full_self = (
        lax.all_gather(w_neigh, "feat", axis=0, tiled=True),
        lax.all_gather(w_self, "feat", axis=0, tiled=True),
    )
    agg_rows, self_rows = (
        lax.all_to_all(aggregated, "feat", split_axis=1, concat_axis=0, tiled=True),
        lax.all_to_all(own_cols, "feat", split_axis=1, concat_axis=0, tiled=True),
    )
    first_dims = (((0,), (0,)), ((), ()))
    preact = lax.dot_general(agg_rows, full_neigh, first_dims, preferred_element_type=jnp.float32)
    preact = preact + lax.dot_general(
        self_rows, full_self, first_dims, preferred_element_type=jnp.float32
    )
    hidden = jax.nn.silu(preact).astype(jnp.bfloat16)
    gate_sig = jax.nn.sigmoid(preact)
    grad_pre = (
        cotangent[0].astype(jnp.float32) * gate_sig * (1.0 + preact * (1.0 - gate_sig))
    ).astype(jnp.bfloat16)
    grad_scale = float(own_rows * lax.axis_size("node")) ** (-0.5)
    last_dims = (((1,), (1,)), ((), ()))
    term_neigh = jnp.dot(agg_rows, grad_pre, preferred_element_type=jnp.float32)
    term_self = jnp.dot(self_rows, grad_pre, preferred_element_type=jnp.float32)
    share_neigh, share_self = (
        lax.psum_scatter(term_neigh, "feat", scatter_dimension=0, tiled=True),
        lax.psum_scatter(term_self, "feat", scatter_dimension=0, tiled=True),
    )
    total_neigh, total_self = lax.psum((share_neigh, share_self), "node")
    back_agg = lax.dot_general(
        full_neigh, grad_pre, last_dims, preferred_element_type=jnp.float32
    ).astype(jnp.bfloat16)
    back_self = lax.dot_general(
        full_self, grad_pre, last_dims, preferred_element_type=jnp.float32
    ).astype(jnp.bfloat16)
    grad_agg, grad_own = (
        lax.all_to_all(back_agg, "feat", split_axis=0, concat_axis=1, tiled=True),
        lax.all_to_all(back_self, "feat", split_axis=0, concat_axis=1, tiled=True),
    )
    grad_blocks = grad_agg.reshape(feat_dev, row_blocks, tile_side)[:, row_ids, :]
    spread = jnp.einsum("fki,kij->fkj", grad_blocks, tile_vals, preferred_element_type=jnp.float32)
    col_onehot = (col_ids[:, None] == lax.broadcasted_iota(jnp.int32, (1, col_blocks), 1)).astype(
        jnp.float32
    )
    grad_ext = jnp.einsum("fkj,kc->fcj", spread, col_onehot, precision=lax.Precision.HIGHEST)
    grad_ext = grad_ext.reshape(feat_dev, col_blocks * tile_side)
    outgoing = grad_ext[:, own_rows:].reshape(feat_dev, parts, slots)
    returned = lax.all_to_all(outgoing, "node", split_axis=1, concat_axis=1, tiled=True)
    returned = jnp.where(live_slots[None], returned, jnp.zeros((), returned.dtype))
    grad_cols = grad_ext[:, :own_rows] + grad_own.astype(jnp.float32)
    grad_cols = grad_cols.at[:, targets.reshape(-1)].add(returned.reshape(feat_dev, parts * slots))
    return (
        hidden[None],
        grad_cols.astype(jnp.bfloat16)[None],
        total_neigh * grad_scale,
        total_self * grad_scale,
    )


def solution(mesh):
    placed = (
        P("node", "feat", None),
        P("node", None, None, None),
        P("node", None),
        P("node", None),
        P("node", None, None),
        P("node", None),
        P("feat", None),
        P("feat", None),
        P("node", "feat", None),
    )
    return jax.shard_map(
        per_device,
        mesh=mesh,
        in_specs=placed,
        out_specs=(
            P("node", "feat", None),
            P("node", "feat", None),
            P("feat", None),
            P("feat", None),
        ),
        check_vma=False,
    )
```

profile of v0, /device:TPU:1, one launch (start us, length us, event | category | flops | bytes accessed | tf_op | source)
XLA Modules:
  0.0 419.2 jit_solution(5458794064605959569)
XLA Ops:
  11.1 9.1 %gather_fusion = bf16[2048,192]{1,0:T(8,128)(2,1)} fusion(bf16[192,2048]{0,1:T(8,128)(2,1)S(1)} %bitcast.96, s32[2048]{0:T(1024)S(1)} %broadcast_clamp_fusion), kind=kCustom, calls=%fused_computation | custom fusion | bytes 1581056 | tf_op jit(solution)/shard_map/jit(_take)/gather | solution.py:20
  20.3 3.4 select_select_fusion
  23.7 13.0 %all-to-all-start = ((bf16[192,64,32]{0,2,1:T(8,128)(2,1)}), bf16[192,64,32]{0,2,1:T(8,128)(2,1)S(1)}, u32[]{:S(2)}, u32[]{:S(2)}) async-start(bf16[192,64,32]{0,2,1:T(8,128)(2,1)} %select_select_fusion), calls=%async_computation | async-start | bytes 2097152 | tf_op jit(solution)/shard_map/all_to_all | solution.py:22
  38.7 26.5 %all-to-all-done = bf16[192,64,32]{0,2,1:T(8,128)(2,1)S(1)} async-done(((bf16[192,64,32]{0,2,1:T(8,128)(2,1)}), bf16[192,64,32]{0,2,1:T(8,128)(2,1)S(1)}, u32[]{:S(2)}, u32[]{:S(2)}) %all-to-all-start) | async-done | bytes 786464 | tf_op jit(solution)/shard_map/all_to_all | solution.py:22
  73.2 5.2 %fusion.26 = bf16[192,16,128]{2,1,0:T(8,128)(2,1)} fusion(f32[192,48,128]{2,0,1:T(8,128)S(1)} %fusion.8, s32[48]{0:T(128)S(1)} %bitcast.112), kind=kOutput, calls=%fused_computation.32 | convolution fusion | flops 226886400 | bytes 5505216 | tf_op jit(solution)/shard_map/fki,kr->fri/dot_general | solution.py:33
  81.3 4.2 all-to-all-start.1
  89.1 8.4 %all-to-all-done.1 = bf16[192,4,512]{2,0,1:T(8,128)(2,1)S(1)} async-done(((bf16[192,4,512]{2,0,1:T(8,128)(2,1)}), bf16[192,4,512]{2,0,1:T(8,128)(2,1)S(1)}, u32[]{:S(2)}, u32[]{:S(2)}) %all-to-all-start.1) | async-done | bytes 786464 | tf_op jit(solution)/shard_map/all_to_all | solution.py:42
  97.5 3.5 all-to-all-start.2
  101.3 3.8 fusion.39
  105.0 7.1 %all-to-all-done.2 = bf16[192,4,512]{2,0,1:T(8,128)(2,1)S(1)} async-done(((bf16[192,4,512]{2,0,1:T(8,128)(2,1)}), bf16[192,4,512]{2,0,1:T(8,128)(2,1)S(1)}, u32[]{:S(2)}, u32[]{:S(2)}) %all-to-all-start.2) | async-done | bytes 786464 | tf_op jit(solution)/shard_map/all_to_all | solution.py:43
  112.1 5.1 %fusion.15 = (bf16[512,1024]{1,0:T(8,128)(2,1)S(1)}, bf16[1,512,1024]{2,1,0:T(8,128)(2,1)}) fusion(bf16[1,512,1024]{2,1,0:T(8,128)(2,1)} %param.17, f32[512,1024]{1,0:T(8,128)} %fusion.39, bf16[768,512]{1,0:T(8,128)(2,1)S(1)} %bitcast.103, bf16[768,1024]{1,0:T(8,128)(2,1)} %all-gather.5.cloned.1.call-done), kind=kOutput, calls=%fused_computation.17 | convolution fusion | flops 812122112 | bytes 7602176 | tf_op jit(solution)/shard_map/dot_general | solution.py:47
  128.5 3.5 all-to-all-start.3
  132.0 3.3 fusion.25
  137.7 14.7 %all-to-all-done.3 = bf16[4,192,512]{2,1,0:T(8,128)(2,1)S(1)} async-done(((bf16[4,192,512]{2,1,0:T(8,128)(2,1)}), bf16[4,192,512]{2,1,0:T(8,128)(2,1)S(1)}, u32[]{:S(2)}, u32[]{:S(2)}) %all-to-all-start.3) | async-done | bytes 786464 | tf_op jit(solution)/shard_map/all_to_all | solution.py:71
  152.4 4.4 %all-to-all-start.4 = ((bf16[4,192,512]{2,1,0:T(8,128)(2,1)}), bf16[4,192,512]{2,1,0:T(8,128)(2,1)}, u32[]{:S(2)}, u32[]{:S(2)}) async-start(bf16[4,192,512]{2,1,0:T(8,128)(2,1)} %bitcast.32), calls=%async_computation.4 | async-start | bytes 1572864 | tf_op jit(solution)/shard_map/all_to_all | solution.py:72
  164.7 6.5 %fusion.16 = f32[192,32,128]{2,1,0:T(8,128)} fusion(f32[192,48,128]{2,0,1:T(8,128)S(1)} %fusion.11, s32[48]{0:T(128)S(1)} %bitcast.113), kind=kOutput, calls=%fused_computation.20 | convolution fusion | flops 452986368 | bytes 7864512 | tf_op jit(solution)/shard_map/fkj,kc->fcj/dot_general | solution.py:79
  171.3 5.0 %copy.71 = f32[192,32,128]{0,2,1:T(8,128)} copy(f32[192,32,128]{2,1,0:T(8,128)} %fusion.16) | data formatting | bytes 6291456 | tf_op jit(solution)/shard_map/reshape | solution.py:80
  179.4 5.3 %fusion.38 = (f32[192,2048]{0,1:T(8,128)}, f32[192,2048]{0,1:T(8,128)}) fusion(f32[192,4096]{0,1:T(8,128)} %bitcast.97, f32[192,4,512]{0,2,1:T(8,128)} %copy.66), kind=kLoop, calls=%fused_computation.56 | loop fusion | flops 393216 | bytes 7864320 | tf_op jit(solution)/shard_map/slice | solution.py:81
  184.7 9.5 %all-to-all-start.5 = ((f32[192,64,32]{0,2,1:T(8,128)}), f32[192,64,32]{0,2,1:T(8,128)}, u32[]{:S(2)}, u32[]{:S(2)}) async-start(f32[192,64,32]{0,2,1:T(8,128)} %bitcast.98), calls=%async_computation.5 | async-start | bytes 4194304 | tf_op jit(solution)/shard_map/all_to_all | solution.py:82
  194.5 22.7 %reduce-scatter.5.cloned.1.call-done = f32[192,1024]{1,0:T(8,128)} async-done(((f32[768,1024]{1,0:T(8,128)}), f32[192,1024]{1,0:T(8,128)}) %reduce-scatter.5.cloned.1.call-update) | async-done | bytes 786448 | tf_op jit(solution)/shard_map/reduce_scatter | solution.py:61
  217.2 29.0 %all-to-all-done.5 = f32[192,64,32]{0,2,1:T(8,128)} async-done(((f32[192,64,32]{0,2,1:T(8,128)}), f32[192,64,32]{0,2,1:T(8,128)}, u32[]{:S(2)}, u32[]{:S(2)}) %all-to-all-start.5) | async-done | bytes 1572896 | tf_op jit(solution)/shard_map/all_to_all | solution.py:82
  246.2 3.2 broadcast_select_fusion
  249.4 14.9 %scatter_fusion = f32[192,2048]{0,1:T(8,128)} fusion(f32[192,2048]{0,1:T(8,128)} %get-tuple-element.23, s32[2048]{0:T(1024)S(1)} %bitcast.111, f32[2048,192]{1,0:T(8,128)} %bitcast.100), kind=kCustom, calls=%fused_computation.3 | custom fusion | flops 393216 | bytes 4726784 | tf_op jit(solution)/shard_map/scatter-add | solution.py:85
  267.2 142.6 %all-reduce.3.cloned.1.call-done = (f32[192,1024]{1,0:T(8,128)}, f32[192,1024]{1,0:T(8,128)}) async-done(((f32[192,1024]{1,0:T(8,128)}, f32[192,1024]{1,0:T(8,128)}), (f32[192,1024]{1,0:T(8,128)}, f32[192,1024]{1,0:T(8,128)})) %all-reduce.3.cloned.1.call-update) | async-done | bytes 1572880 | tf_op jit(solution)/shard_map/psum | solution.py:63
  (67 shorter events, 51.2 us)
Async XLA Ops:
  7.2 63.2 %copy-start = (bf16[1,48,128,128]{3,2,1,0:T(8,128)(2,1)S(1)}, bf16[1,48,128,128]{3,2,1,0:T(8,128)(2,1)}, u32[]{:S(2)}) copy-start(bf16[1,48,128,128]{3,2,1,0:T(8,128)(2,1)} %param.10) | copy-start | bytes 4718596
  7.2 94.1 %all-gather.3.cloned.1.call-start = ((), (), s32[]{:S(2)}) async-start(), calls=%async_computation.8 | async-start | bytes 1966080 | tf_op jit(solution)/shard_map/all_gather | solution.py:38
  11.1 9.1 %copy-start.7 = (s32[1,64]{1,0:T(1,128)S(1)}, s32[1,64]{1,0:T(1,128)}, u32[]{:S(2)}) copy-start(s32[1,64]{1,0:T(1,128)} %param.14) | copy-start | bytes 772
  20.2 17.2 %copy-start.6 = (s32[1,48]{1,0:T(1,128)S(1)}, s32[1,48]{1,0:T(1,128)}, u32[]{:S(2)}) copy-start(s32[1,48]{1,0:T(1,128)} %param.12) | copy-start | bytes 580
  20.3 17.2 %copy-start.1 = (bf16[1,192,2048]{2,1,0:T(8,128)(2,1)S(1)}, bf16[1,192,2048]{2,1,0:T(8,128)(2,1)}, u32[]{:S(2)}) copy-start(bf16[1,192,2048]{2,1,0:T(8,128)(2,1)} %param.9) | copy-start | bytes 2359300
  23.7 41.6 %all-to-all-start = ((bf16[192,64,32]{0,2,1:T(8,128)(2,1)}), bf16[192,64,32]{0,2,1:T(8,128)(2,1)S(1)}, u32[]{:S(2)}, u32[]{:S(2)}) async-start(bf16[192,64,32]{0,2,1:T(8,128)(2,1)} %select_select_fusion), calls=%async_computation | async-start | bytes 2097152 | tf_op jit(solution)/shard_map/all_to_all | solution.py:22
  36.7 75.4 %all-gather.5.cloned.1.call-start = ((), (), s32[]{:S(2)}) async-start(), calls=%async_computation.9 | async-start | bytes 1966080 | tf_op jit(solution)/shard_map/all_gather | solution.py:39
  70.4 2.8 copy-start.5
  78.4 7.0 %copy-start.2 = (bf16[1,192,2048]{2,1,0:T(8,128)(2,1)S(1)}, bf16[1,192,2048]{2,1,0:T(8,128)(2,1)}, u32[]{:S(2)}) copy-start(bf16[1,192,2048]{2,1,0:T(8,128)(2,1)} %param.9) | copy-start | bytes 2359300
  81.3 16.2 %all-to-all-start.1 = ((bf16[192,4,512]{2,0,1:T(8,128)(2,1)}), bf16[192,4,512]{2,0,1:T(8,128)(2,1)S(1)}, u32[]{:S(2)}, u32[]{:S(2)}) async-start(bf16[192,4,512]{2,0,1:T(8,128)(2,1)} %copy.58), calls=%async_computation.1 | async-start | bytes 1572864 | tf_op jit(solution)/shard_map/all_to_all | solution.py:42
  97.5 14.6 %all-to-all-start.2 = ((bf16[192,4,512]{2,0,1:T(8,128)(2,1)}), bf16[192,4,512]{2,0,1:T(8,128)(2,1)S(1)}, u32[]{:S(2)}, u32[]{:S(2)}) async-start(bf16[192,4,512]{2,0,1:T(8,128)(2,1)} %copy.59), calls=%async_computation.2 | async-start | bytes 1572864 | tf_op jit(solution)/shard_map/all_to_all | solution.py:43
  101.0 93.5 %reduce-scatter.3.cloned.1.call-start = ((), (), s32[]{:S(2)}) async-start(), calls=%async_computation.10 | async-start | bytes 3932160 | tf_op jit(solution)/shard_map/reduce_scatter | solution.py:60
  117.3 1.0 copy-start.3
  120.9 1.2 copy-start.4
  121.0 96.2 %reduce-scatter.5.cloned.1.call-start = ((), (), s32[]{:S(2)}) async-start(), calls=%async_computation.11 | async-start | bytes 3932160 | tf_op jit(solution)/shard_map/reduce_scatter | solution.py:61
  128.5 23.9 %all-to-all-start.3 = ((bf16[4,192,512]{2,1,0:T(8,128)(2,1)}), bf16[4,192,512]{2,1,0:T(8,128)(2,1)S(1)}, u32[]{:S(2)}, u32[]{:S(2)}) async-start(bf16[4,192,512]{2,1,0:T(8,128)(2,1)} %bitcast.108), calls=%async_computation.3 | async-start | bytes 1572864 | tf_op jit(solution)/shard_map/all_to_all | solution.py:71
  152.4 23.9 %all-to-all-start.4 = ((bf16[4,192,512]{2,1,0:T(8,128)(2,1)}), bf16[4,192,512]{2,1,0:T(8,128)(2,1)}, u32[]{:S(2)}, u32[]{:S(2)}) async-start(bf16[4,192,512]{2,1,0:T(8,128)(2,1)} %bitcast.32), calls=%async_computation.4 | async-start | bytes 1572864 | tf_op jit(solution)/shard_map/all_to_all | solution.py:72
  184.7 61.5 %all-to-all-start.5 = ((f32[192,64,32]{0,2,1:T(8,128)}), f32[192,64,32]{0,2,1:T(8,128)}, u32[]{:S(2)}, u32[]{:S(2)}) async-start(f32[192,64,32]{0,2,1:T(8,128)} %bitcast.98), calls=%async_computation.5 | async-start | bytes 4194304 | tf_op jit(solution)/shard_map/all_to_all | solution.py:82
  194.2 215.7 %all-reduce.3.cloned.1.call-start = ((), (), s32[]{:S(2)}) async-start(), calls=%async_computation.12 | async-start | bytes 3145728 | tf_op jit(solution)/shard_map/psum | solution.py:63
Sparse Core Ops, SparseCore 0:
  9.8 32.8 all-gather.2
  44.6 29.1 all-gather.4
  121.1 50.4 reduce-scatter.2
  174.0 43.1 reduce-scatter.4
  220.5 189.3 all-reduce.2
where the time goes:
time: 421 us; the launch traced here: 419 us
  waiting for transfers between devices  253 us (60%)
  local copies, waits for them, and re-layouts  41.9 us (10%)
  starting transfers between devices  38.7 us (9%)
  matrix products  37 us (9%)
  other arithmetic  35 us (8%)
  between operations  14 us (3%)
    psum x1, waiting for transfers between devices, per_device(): total_neigh, total_self = lax.psum((share_neigh, share_self), 'node')  143 us
    all_to_all x1, waiting for transfers between devices, per_device(): lax.all_to_all(outgoing, 'node', split_axis=1, concat_axis=1, tiled=True)  29 us
    all_to_all x1, waiting for transfers between devices, per_device(): lax.all_to_all(picked, 'node', split_axis=1, concat_axis=1, tiled=True)  26.5 us
    reduce_scatter x1, waiting for transfers between devices, per_device(): lax.psum_scatter(term_self, 'feat', scatter_dimension=0, tiled=True)  22.7 us
    scatter-add x1, other arithmetic, per_device(): grad_cols.at[:, targets.reshape(-1)]  14.9 us
    all_to_all x1, waiting for transfers between devices, per_device(): lax.all_to_all(back_agg, 'feat', split_axis=0, concat_axis=1, tiled=True)  14.7 us
    all_to_all x1, starting transfers between devices, per_device(): lax.all_to_all(picked, 'node', split_axis=1, concat_axis=1, tiled=True)  13 us
    all_to_all x1, starting transfers between devices, per_device(): lax.all_to_all(outgoing, 'node', split_axis=1, concat_axis=1, tiled=True)  9.45 us
  transfers between devices with their start and end apart: 11, of which 7 were waited for; matrix products, arithmetic and copies ran while one was open for 24% of the time, Pallas kernels for 0%

commit v1 on v0

--- a/solution.py
+++ b/solution.py
@@ -1,7 +1,164 @@
+import functools
+
 import jax
 import jax.numpy as jnp
 from jax import lax
+from jax.experimental import pallas as pl
+from jax.experimental.pallas import tpu as pltpu
 from jax.sharding import PartitionSpec as P
+
+NX, NY, NZ, NC = 4, 4, 8, 2
+MESH = pl.DeviceIdType.MESH
+
+
+def place():
+    n = lax.axis_index("node")
+    y = lax.axis_index("feat")
+    return lax.div(n, NZ * NC), y, lax.rem(lax.div(n, NC), NZ), lax.rem(n, NC)
+
+
+def node_id(x, z, c):
+    return {"node": (x * NZ + z) * NC + c}
+
+
+def remote(src, dst, send, recv, device):
+    return pltpu.make_async_remote_copy(
+        src_ref=src, dst_ref=dst, send_sem=send, recv_sem=recv, device_id=device, device_id_type=MESH
+    )
+
+
+def total_kernel(
+    scale, term_ref, out_ref,
+    core_in, sum1, y_in, sum2, x_in, sum3, z_in, sum4, strip, rows, other,
+    core_sem, y_send, y_recv, x_send, x_recv, z_send, z_recv, zg_send, zg_recv, xg_send, xg_recv, cg_sem,
+):
+    x, y, z, c = place()
+    feat = out_ref.shape[1]
+    xr = feat // NX
+    zc = out_ref.shape[2] // NZ
+    partner = node_id(x, z, 1 - c)
+    y_peer = lambda d: {"feat": lax.rem(y + d, NY)}
+    x_peer = lambda d: node_id(lax.rem(x + d, NX), z, c)
+    z_peer = lambda d: node_id(x, lax.rem(z + d, NZ), c)
+
+    barrier = pltpu.get_barrier_semaphore()
+    pl.semaphore_signal(barrier, inc=1, device_id=partner, device_id_type=MESH)
+    for d in range(1, NY):
+        pl.semaphore_signal(barrier, inc=1, device_id=y_peer(d), device_id_type=MESH)
+    for d in range(1, NX):
+        pl.semaphore_signal(barrier, inc=1, device_id=x_peer(d), device_id_type=MESH)
+    for d in range(1, NZ):
+        pl.semaphore_signal(barrier, inc=1, device_id=z_peer(d), device_id_type=MESH)
+    pl.semaphore_wait(barrier, 1 + NY - 1 + NX - 1 + NZ - 1)
+
+    f32 = jnp.float32
+    bf16 = jnp.bfloat16
+    swap = remote(term_ref.at[1 - c], core_in, core_sem.at[0], core_sem.at[1], partner)
+    swap.start()
+    swap.wait()
+
+    y_copies = []
+    for d in range(1, NY):
+        q = lax.rem(y + d, NY)
+        sum1[q] = (term_ref[c, q].astype(f32) + core_in[q].astype(f32)).astype(bf16)
+        cp = remote(sum1.at[q], y_in.at[d - 1], y_send.at[d - 1], y_recv.at[d - 1], y_peer(d))
+        cp.start()
+        y_copies.append(cp)
+    acc = term_ref[c, y].astype(f32) + core_in[y].astype(f32)
+    for cp in y_copies:
+        cp.wait()
+    for d in range(1, NY):
+        acc = acc + y_in[d - 1].astype(f32)
+    acc = acc.reshape(NX, xr, acc.shape[1])
+    sum2[...] = acc.astype(bf16)
+
+    x_copies = []
+    for d in range(1, NX):
+        q = lax.rem(x + d, NX)
+        cp = remote(sum2.at[q], x_in.at[d - 1], x_send.at[d - 1], x_recv.at[d - 1], x_peer(d))
+        cp.start()
+        x_copies.append(cp)
+    for cp in x_copies:
+        cp.wait()
+    acc = sum2[x].astype(f32)
+    for d in range(1, NX):
+        acc = acc + x_in[d - 1].astype(f32)
+    for q in range(NZ):
+        sum3[q] = acc[:, q * zc:(q + 1) * zc].astype(bf16)
+
+    z_copies = []
+    for d in range(1, NZ):
+        q = lax.rem(z + d, NZ)
+        cp = remote(sum3.at[q], z_in.at[d - 1], z_send.at[d - 1], z_recv.at[d - 1], z_peer(d))
+        cp.start()
+        z_copies.append(cp)
+    for cp in z_copies:
+        cp.wait()
+    acc = sum3[z].astype(f32)
+    for d in range(1, NZ):
+        acc = acc + z_in[d - 1].astype(f32)
+    sum4[...] = acc.astype(bf16)
+
+    z_copies = []
+    for d in range(1, NZ):
+        cp = remote(sum4, strip.at[z], zg_send.at[d - 1], zg_recv.at[d - 1], z_peer(d))
+        cp.start()
+        z_copies.append(cp)
+    strip[z] = sum4[...]
+    for cp in z_copies:
+        cp.wait()
+
+    x_copies = []
+    for d in range(1, NX):
+        cp = remote(strip, rows.at[x], xg_send.at[d - 1], xg_recv.at[d - 1], x_peer(d))
+        cp.start()
+        x_copies.append(cp)
+    rows[x] = strip[...]
+    for cp in x_copies:
+        cp.wait()
+
+    back = remote(rows, other, cg_sem.at[0], cg_sem.at[1], partner)
+    back.start()
+    for a in range(NX):
+        for b in range(NZ):
+            out_ref[c, a * xr:(a + 1) * xr, b * zc:(b + 1) * zc] = rows[a, b].astype(f32) * scale
+    back.wait()
+    for a in range(NX):
+        for b in range(NZ):
+            out_ref[1 - c, a * xr:(a + 1) * xr, b * zc:(b + 1) * zc] = other[a, b].astype(f32) * scale
+
+
+def total_grads(terms, scale):
+    _, parts, feat, hid = terms.shape
+    xr, zc = feat // NX, hid // NZ
+    bf16 = jnp.bfloat16
+    dma = pltpu.SemaphoreType.DMA
+    return pl.pallas_call(
+        functools.partial(total_kernel, scale),
+        out_shape=jax.ShapeDtypeStruct((NC, feat, hid), jnp.float32),
+        in_specs=[pl.BlockSpec(memory_space=pltpu.VMEM)],
+        out_specs=pl.BlockSpec(memory_space=pltpu.VMEM),
+        scratch_shapes=[
+            pltpu.VMEM((parts, feat, hid), bf16),
+            pltpu.VMEM((parts, feat, hid), bf16),
+            pltpu.VMEM((NY - 1, feat, hid), bf16),
+            pltpu.VMEM((NX, xr, hid), bf16),
+            pltpu.VMEM((NX - 1, xr, hid), bf16),
+            pltpu.VMEM((NZ, xr, zc), bf16),
+            pltpu.VMEM((NZ - 1, xr, zc), bf16),
+            pltpu.VMEM((xr, zc), bf16),
+            pltpu.VMEM((NZ, xr, zc), bf16),
+            pltpu.VMEM((NX, NZ, xr, zc), bf16),
+            pltpu.VMEM((NX, NZ, xr, zc), bf16),
+            dma((2,)), dma((NY - 1,)), dma((NY - 1,)), dma((NX - 1,)), dma((NX - 1,)),
+            dma((NZ - 1,)), dma((NZ - 1,)), dma((NZ - 1,)), dma((NZ - 1,)),
+            dma((NX - 1,)), dma((NX - 1,)), dma((2,)),
+        ],
+        compiler_params=pltpu.CompilerParams(
+            collective_id=0, has_side_effects=True, vmem_limit_bytes=48 << 20
+        ),
+        name="total_grads",
+    )(terms)
 
 
 def per_device(
@@ -56,11 +213,8 @@
     last_dims = (((1,), (1,)), ((), ()))
     term_neigh = jnp.dot(agg_rows, grad_pre, preferred_element_type=jnp.float32)
     term_self = jnp.dot(self_rows, grad_pre, preferred_element_type=jnp.float32)
-    share_neigh, share_self = (
-        lax.psum_scatter(term_neigh, "feat", scatter_dimension=0, tiled=True),
-        lax.psum_scatter(term_self, "feat", scatter_dimension=0, tiled=True),
-    )
-    total_neigh, total_self = lax.psum((share_neigh, share_self), "node")
+    terms = jnp.stack([term_neigh.astype(jnp.bfloat16), term_self.astype(jnp.bfloat16)])
+    totals = total_grads(terms.reshape(NC, NY, feat_dev, terms.shape[-1]), grad_scale)
     back_agg = lax.dot_general(
         full_neigh, grad_pre, last_dims, preferred_element_type=jnp.float32
     ).astype(jnp.bfloat16)
@@ -86,8 +240,8 @@
     return (
         hidden[None],
         grad_cols.astype(jnp.bfloat16)[None],
-        total_neigh * grad_scale,
-        total_self * grad_scale,
+        totals[0],
+        totals[1],
     )
 
 

time: 421 us -> 283 us (0.67)
  waiting for transfers between devices: 253 us -> 56.9 us
  Pallas kernels: 0 us -> 62.3 us
    psum x1 -> x0, waiting for transfers between devices: 143 us -> none  [per_device(): total_neigh, total_self = lax.psum((share_neigh, share_self), 'node')]
    pallas_call x0 -> x1, Pallas kernels: none -> 62.3 us  [total_grads(): pl.pallas_call(functools.partial(total_kernel, scale), out_shape=jax.Shap...]
    all_to_all x1, waiting for transfers between devices: 29 us -> 0.01 us  [per_device(): lax.all_to_all(outgoing, 'node', split_axis=1, concat_axis=1, tiled=True)]
    reduce_scatter x2 -> x0, waiting for transfers between devices: 22.7 us -> none  [the longest x1 22.7 us: per_device(): lax.psum_scatter(term_self, 'feat', scatter_dimension=0, tiled=True)]
    all_to_all x1, waiting for transfers between devices: 14.7 us -> 5.96 us  [per_device(): lax.all_to_all(back_agg, 'feat', split_axis=0, concat_axis=1, tiled=True)]
    all_to_all x1, waiting for transfers between devices: 0.01 us -> 5.6 us  [per_device(): lax.all_to_all(back_self, 'feat', split_axis=0, concat_axis=1, tiled=True)]
  transfers between devices with their start and end apart: 11 -> 8, of which waited for: 7 -> 5; matrix products, arithmetic and copies ran while one was open for 24% -> 18% of each run, Pallas kernels for 0% -> 22%
where the time goes in v1:
time: 283 us; the launch traced here: 282 us
  Pallas kernels  62.3 us (22%)
  waiting for transfers between devices  56.9 us (20%)
  starting transfers between devices  41.1 us (15%)
  local copies, waits for them, and re-layouts  40 us (14%)
  other arithmetic  33.8 us (12%)
  matrix products  33.2 us (12%)
  between operations  14.3 us (5%)
    pallas_call x1, Pallas kernels, total_grads(): pl.pallas_call(functools.partial(total_kernel, scale), out_shape=jax.Shap...  62.3 us
    all_to_all x1, waiting for transfers between devices, per_device(): lax.all_to_all(picked, 'node', split_axis=1, concat_axis=1, tiled=True)  26.5 us
    scatter-add x1, other arithmetic, per_device(): grad_cols.at[:, targets.reshape(-1)]  15 us
    all_to_all x1, starting transfers between devices, per_device(): lax.all_to_all(picked, 'node', split_axis=1, concat_axis=1, tiled=True)  13 us
    all_to_all x1, starting transfers between devices, per_device(): lax.all_to_all(outgoing, 'node', split_axis=1, concat_axis=1, tiled=True)  12.5 us
    all_to_all x1, waiting for transfers between devices, per_device(): lax.all_to_all(aggregated, 'feat', split_axis=1, concat_axis=0, tiled=True)  10.5 us
    gather x1, local copies, waits for them, and re-layouts, per_device(): jnp.take(own_cols, targets.reshape(-1), axis=1)  9.06 us
    all_to_all x1, waiting for transfers between devices, per_device(): lax.all_to_all(own_cols, 'feat', split_axis=1, concat_axis=0, tiled=True)  6.88 us
  transfers between devices with their start and end apart: 8, of which 5 were waited for; matrix products, arithmetic and copies ran while one was open for 18% of the time, Pallas kernels for 22%

profile of v1, /device:TPU:1, one launch (start us, length us, event | category | flops | bytes accessed | tf_op | source)
XLA Modules:
  0.0 281.7 jit_solution(4888528611476981894)
XLA Ops:
  11.1 9.1 %gather_fusion = bf16[2048,192]{1,0:T(8,128)(2,1)} fusion(bf16[192,2048]{0,1:T(8,128)(2,1)S(1)} %bitcast.102, s32[2048]{0:T(1024)S(1)} %broadcast_clamp_fusion), kind=kCustom, calls=%fused_computation | custom fusion | bytes 1581056 | tf_op jit(solution)/shard_map/jit(_take)/gather | solution.py:177
  20.3 3.4 %select_select_fusion = bf16[192,64,32]{0,2,1:T(8,128)(2,1)} fusion(bf16[192,64,32]{0,2,1:T(8,128)(2,1)} %bitcast.108, pred[64,32]{1,0:T(8,128)(4,1)S(1)} %copy.49, pred[64,32]{1,0:T(8,128)(4,1)S(1)} %iota_compare_fusion), kind=kLoop, calls=%fused_computation.37 | loop fusion | flops 786432 | bytes 1576960 | tf_op jit(solution)/shard_map/jit(_where)/select_n | solution.py:178
  23.7 13.0 %all-to-all-start = ((bf16[192,64,32]{0,2,1:T(8,128)(2,1)}), bf16[192,64,32]{0,2,1:T(8,128)(2,1)S(1)}, u32[]{:S(2)}, u32[]{:S(2)}) async-start(bf16[192,64,32]{0,2,1:T(8,128)(2,1)} %select_select_fusion), calls=%async_computation | async-start | bytes 2097152 | tf_op jit(solution)/shard_map/all_to_all | solution.py:179
  38.7 26.5 %all-to-all-done = bf16[192,64,32]{0,2,1:T(8,128)(2,1)S(1)} async-done(((bf16[192,64,32]{0,2,1:T(8,128)(2,1)}), bf16[192,64,32]{0,2,1:T(8,128)(2,1)S(1)}, u32[]{:S(2)}, u32[]{:S(2)}) %all-to-all-start) | async-done | bytes 786464 | tf_op jit(solution)/shard_map/all_to_all | solution.py:179
  70.4 2.8 fusion.8
  73.2 5.2 %fusion.26 = bf16[192,16,128]{2,1,0:T(8,128)(2,1)} fusion(f32[192,48,128]{2,0,1:T(8,128)S(1)} %fusion.8, s32[48]{0:T(128)S(1)} %bitcast.117), kind=kOutput, calls=%fused_computation.34 | convolution fusion | flops 226886400 | bytes 5505216 | tf_op jit(solution)/shard_map/fki,kr->fri/dot_general | solution.py:190
  81.3 4.2 %all-to-all-start.1 = ((bf16[192,4,512]{2,0,1:T(8,128)(2,1)}), bf16[192,4,512]{2,0,1:T(8,128)(2,1)}, u32[]{:S(2)}, u32[]{:S(2)}) async-start(bf16[192,4,512]{2,0,1:T(8,128)(2,1)} %copy.55), calls=%async_computation.1 | async-start | bytes 1572864 | tf_op jit(solution)/shard_map/all_to_all | solution.py:199
  87.1 10.5 %all-to-all-done.1 = bf16[192,4,512]{2,0,1:T(8,128)(2,1)} async-done(((bf16[192,4,512]{2,0,1:T(8,128)(2,1)}), bf16[192,4,512]{2,0,1:T(8,128)(2,1)}, u32[]{:S(2)}, u32[]{:S(2)}) %all-to-all-start.1) | async-done | bytes 786464 | tf_op jit(solution)/shard_map/all_to_all | solution.py:199
  97.6 3.7 %all-to-all-start.2 = ((bf16[192,4,512]{2,0,1:T(8,128)(2,1)}), bf16[192,4,512]{2,0,1:T(8,128)(2,1)S(1)}, u32[]{:S(2)}, u32[]{:S(2)}) async-start(bf16[192,4,512]{2,0,1:T(8,128)(2,1)} %copy.56), calls=%async_computation.2 | async-start | bytes 1572864 | tf_op jit(solution)/shard_map/all_to_all | solution.py:200
  101.3 4.0 %fusion.39 = f32[512,1024]{1,0:T(8,128)} fusion(bf16[768,512]{1,0:T(8,128)(2,1)} %bitcast.16, bf16[768,1024]{1,0:T(8,128)(2,1)} %all-gather.3.cloned.1.call-done), kind=kOutput, calls=%fused_computation.59 | convolution fusion | flops 805306368 | bytes 4456448 | tf_op jit(solution)/shard_map/dot_general | solution.py:203
  105.4 6.9 %all-to-all-done.2 = bf16[192,4,512]{2,0,1:T(8,128)(2,1)S(1)} async-done(((bf16[192,4,512]{2,0,1:T(8,128)(2,1)}), bf16[192,4,512]{2,0,1:T(8,128)(2,1)S(1)}, u32[]{:S(2)}, u32[]{:S(2)}) %all-to-all-start.2) | async-done | bytes 786464 | tf_op jit(solution)/shard_map/all_to_all | solution.py:200
  112.2 5.4 %fusion.15 = (bf16[512,1024]{1,0:T(8,128)(2,1)S(1)}, bf16[1,512,1024]{2,1,0:T(8,128)(2,1)}) fusion(bf16[1,512,1024]{2,1,0:T(8,128)(2,1)} %param.17, f32[512,1024]{1,0:T(8,128)} %fusion.39, bf16[768,512]{1,0:T(8,128)(2,1)S(1)} %bitcast.113, bf16[768,1024]{1,0:T(8,128)(2,1)} %all-gather.5.cloned.1.call-done), kind=kOutput, calls=%fused_computation.18 | convolution fusion | flops 812122112 | bytes 7602176 | tf_op jit(solution)/shard_map/dot_general | solution.py:204
  120.9 3.5 %all-to-all-start.3 = ((bf16[4,192,512]{2,1,0:T(8,128)(2,1)}), bf16[4,192,512]{2,1,0:T(8,128)(2,1)S(1)}, u32[]{:S(2)}, u32[]{:S(2)}) async-start(bf16[4,192,512]{2,1,0:T(8,128)(2,1)} %bitcast.24), calls=%async_computation.3 | async-start | bytes 1572864 | tf_op jit(solution)/shard_map/all_to_all | solution.py:225
  128.3 6.0 %all-to-all-done.3 = bf16[4,192,512]{2,1,0:T(8,128)(2,1)S(1)} async-done(((bf16[4,192,512]{2,1,0:T(8,128)(2,1)}), bf16[4,192,512]{2,1,0:T(8,128)(2,1)S(1)}, u32[]{:S(2)}, u32[]{:S(2)}) %all-to-all-start.3) | async-done | bytes 786464 | tf_op jit(solution)/shard_map/all_to_all | solution.py:225
  134.3 4.2 %all-to-all-start.4 = ((bf16[4,192,512]{2,1,0:T(8,128)(2,1)}), bf16[4,192,512]{2,1,0:T(8,128)(2,1)}, u32[]{:S(2)}, u32[]{:S(2)}) async-start(bf16[4,192,512]{2,1,0:T(8,128)(2,1)} %bitcast.32), calls=%async_computation.4 | async-start | bytes 1572864 | tf_op jit(solution)/shard_map/all_to_all | solution.py:226
  141.7 5.6 %all-to-all-done.4 = bf16[4,192,512]{2,1,0:T(8,128)(2,1)} async-done(((bf16[4,192,512]{2,1,0:T(8,128)(2,1)}), bf16[4,192,512]{2,1,0:T(8,128)(2,1)}, u32[]{:S(2)}, u32[]{:S(2)}) %all-to-all-start.4) | async-done | bytes 786464 | tf_op jit(solution)/shard_map/all_to_all | solution.py:226
  149.8 2.9 %copy.63 = f32[192,4,512]{0,2,1:T(8,128)} copy(f32[192,4,512]{2,0,1:T(8,128)} %convert_bitcast_fusion) | data formatting | bytes 3145728 | tf_op jit(solution)/shard_map/convert_element_type | solution.py:238
  157.5 6.5 %fusion.16 = f32[192,32,128]{2,1,0:T(8,128)} fusion(f32[192,48,128]{2,0,1:T(8,128)S(1)} %fusion.11, s32[48]{0:T(128)S(1)} %bitcast.118), kind=kOutput, calls=%fused_computation.21 | convolution fusion | flops 452986368 | bytes 7864512 | tf_op jit(solution)/shard_map/fkj,kc->fcj/dot_general | solution.py:233
  163.9 5.0 %copy.66 = f32[192,32,128]{0,2,1:T(8,128)} copy(f32[192,32,128]{2,1,0:T(8,128)} %fusion.16) | data formatting | bytes 6291456 | tf_op jit(solution)/shard_map/reshape | solution.py:234
  168.9 5.2 %fusion.38 = (f32[192,2048]{0,1:T(8,128)}, f32[192,2048]{0,1:T(8,128)}) fusion(f32[192,4096]{0,1:T(8,128)} %bitcast.103, f32[192,4,512]{0,2,1:T(8,128)} %copy.63), kind=kLoop, calls=%fused_computation.58 | loop fusion | flops 393216 | bytes 7864320 | tf_op jit(solution)/shard_map/slice | solution.py:235
  174.1 12.5 %all-to-all-start.5 = ((f32[192,64,32]{0,2,1:T(8,128)}), f32[192,64,32]{0,2,1:T(8,128)}, u32[]{:S(2)}, u32[]{:S(2)}) async-start(f32[192,64,32]{0,2,1:T(8,128)} %bitcast.104), calls=%async_computation.5 | async-start | bytes 4194304 | tf_op jit(solution)/shard_map/all_to_all | solution.py:236
  190.0 62.3 %total_grads.1 = f32[2,192,1024]{2,1,0:T(8,128)S(1)} custom-call(bf16[2,4,192,1024]{3,2,1,0:T(8,128)(2,1)S(1)} %pad_maximum_fusion.term_ref), custom_call_target="tpu_custom_call" | custom-call | tf_op jit(solution)/shard_map/total_grads/pallas_call | solution.py:136
  253.7 3.3 %broadcast_select_fusion = f32[192,64,32]{0,2,1:T(8,128)} fusion(f32[192,64,32]{0,2,1:T(8,128)} %all-to-all-done.5, pred[64,32]{1,0:T(8,128)(4,1)S(1)} %iota_compare_fusion), kind=kLoop, calls=%fused_computation.36 | loop fusion | flops 393216 | bytes 3147776 | tf_op jit(solution)/shard_map/jit(_where)/select_n | solution.py:237
  256.9 15.0 %scatter_fusion = f32[192,2048]{0,1:T(8,128)} fusion(f32[192,2048]{0,1:T(8,128)} %get-tuple-element.21, s32[2048]{0:T(1024)S(1)} %bitcast.116, f32[2048,192]{1,0:T(8,128)} %bitcast.106), kind=kCustom, calls=%fused_computation.3 | custom fusion | flops 393216 | bytes 4726784 | tf_op jit(solution)/shard_map/scatter-add | solution.py:239
  (68 shorter events, 40.8 us)
Async XLA Ops:
  7.2 63.2 %copy-start = (bf16[1,48,128,128]{3,2,1,0:T(8,128)(2,1)S(1)}, bf16[1,48,128,128]{3,2,1,0:T(8,128)(2,1)}, u32[]{:S(2)}) copy-start(bf16[1,48,128,128]{3,2,1,0:T(8,128)(2,1)} %param.10) | copy-start | bytes 4718596
  7.2 94.2 %all-gather.3.cloned.1.call-start = ((), (), s32[]{:S(2)}) async-start(), calls=%async_computation.6 | async-start | bytes 1966080 | tf_op jit(solution)/shard_map/all_gather | solution.py:195
  11.1 9.1 %copy-start.8 = (s32[1,64]{1,0:T(1,128)S(1)}, s32[1,64]{1,0:T(1,128)}, u32[]{:S(2)}) copy-start(s32[1,64]{1,0:T(1,128)} %param.14) | copy-start | bytes 772
  20.3 17.2 %copy-start.7 = (s32[1,48]{1,0:T(1,128)S(1)}, s32[1,48]{1,0:T(1,128)}, u32[]{:S(2)}) copy-start(s32[1,48]{1,0:T(1,128)} %param.12) | copy-start | bytes 580
  20.3 17.2 %copy-start.2 = (bf16[1,192,2048]{2,1,0:T(8,128)(2,1)S(1)}, bf16[1,192,2048]{2,1,0:T(8,128)(2,1)}, u32[]{:S(2)}) copy-start(bf16[1,192,2048]{2,1,0:T(8,128)(2,1)} %param.9) | copy-start | bytes 2359300
  23.7 41.6 %all-to-all-start = ((bf16[192,64,32]{0,2,1:T(8,128)(2,1)}), bf16[192,64,32]{0,2,1:T(8,128)(2,1)S(1)}, u32[]{:S(2)}, u32[]{:S(2)}) async-start(bf16[192,64,32]{0,2,1:T(8,128)(2,1)} %select_select_fusion), calls=%async_computation | async-start | bytes 2097152 | tf_op jit(solution)/shard_map/all_to_all | solution.py:179
  36.7 75.5 %all-gather.5.cloned.1.call-start = ((), (), s32[]{:S(2)}) async-start(), calls=%async_computation.7 | async-start | bytes 1966080 | tf_op jit(solution)/shard_map/all_gather | solution.py:196
  70.4 2.8 copy-start.6
  78.4 7.1 %copy-start.3 = (bf16[1,192,2048]{2,1,0:T(8,128)(2,1)S(1)}, bf16[1,192,2048]{2,1,0:T(8,128)(2,1)}, u32[]{:S(2)}) copy-start(bf16[1,192,2048]{2,1,0:T(8,128)(2,1)} %param.9) | copy-start | bytes 2359300
  81.3 16.3 %all-to-all-start.1 = ((bf16[192,4,512]{2,0,1:T(8,128)(2,1)}), bf16[192,4,512]{2,0,1:T(8,128)(2,1)}, u32[]{:S(2)}, u32[]{:S(2)}) async-start(bf16[192,4,512]{2,0,1:T(8,128)(2,1)} %copy.55), calls=%async_computation.1 | async-start | bytes 1572864 | tf_op jit(solution)/shard_map/all_to_all | solution.py:199
  97.6 14.6 %all-to-all-start.2 = ((bf16[192,4,512]{2,0,1:T(8,128)(2,1)}), bf16[192,4,512]{2,0,1:T(8,128)(2,1)S(1)}, u32[]{:S(2)}, u32[]{:S(2)}) async-start(bf16[192,4,512]{2,0,1:T(8,128)(2,1)} %copy.56), calls=%async_computation.2 | async-start | bytes 1572864 | tf_op jit(solution)/shard_map/all_to_all | solution.py:200
  112.2 5.4 %copy-start.4 = (bf16[192,4,512]{2,0,1:T(8,128)(2,1)}, bf16[192,4,512]{2,0,1:T(8,128)(2,1)S(1)}, u32[]{:S(2)}) copy-start(bf16[192,4,512]{2,0,1:T(8,128)(2,1)S(1)} %all-to-all-done.2) | copy-start | bytes 2359300
  112.2 6.5 %copy-start.9 = (bf16[768,1024]{1,0:T(8,128)(2,1)S(1)}, bf16[768,1024]{1,0:T(8,128)(2,1)}, u32[]{:S(2)}) copy-start(bf16[768,1024]{1,0:T(8,128)(2,1)} %all-gather.3.cloned.1.call-done) | copy-start | bytes 4718596
  117.7 1.0 copy-start.10
  120.9 13.4 %all-to-all-start.3 = ((bf16[4,192,512]{2,1,0:T(8,128)(2,1)}), bf16[4,192,512]{2,1,0:T(8,128)(2,1)S(1)}, u32[]{:S(2)}, u32[]{:S(2)}) async-start(bf16[4,192,512]{2,1,0:T(8,128)(2,1)} %bitcast.24), calls=%async_computation.3 | async-start | bytes 1572864 | tf_op jit(solution)/shard_map/all_to_all | solution.py:225
  134.3 13.0 %all-to-all-start.4 = ((bf16[4,192,512]{2,1,0:T(8,128)(2,1)}), bf16[4,192,512]{2,1,0:T(8,128)(2,1)}, u32[]{:S(2)}, u32[]{:S(2)}) async-start(bf16[4,192,512]{2,1,0:T(8,128)(2,1)} %bitcast.32), calls=%async_computation.4 | async-start | bytes 1572864 | tf_op jit(solution)/shard_map/all_to_all | solution.py:226
  174.1 12.5 %copy-start.5 = (bf16[192,4,512]{2,0,1:T(8,128)(2,1)S(1)}, bf16[192,4,512]{2,0,1:T(8,128)(2,1)}, u32[]{:S(2)}) copy-start(bf16[192,4,512]{2,0,1:T(8,128)(2,1)} %copy-done.4) | copy-start | bytes 2359300
  174.1 12.5 %copy-start.11 = (bf16[512,1024]{1,0:T(8,128)(2,1)S(1)}, bf16[512,1024]{1,0:T(8,128)(2,1)}, u32[]{:S(2)}) copy-start(bf16[512,1024]{1,0:T(8,128)(2,1)} %copy-done.10) | copy-start | bytes 3145732
  174.1 79.5 %all-to-all-start.5 = ((f32[192,64,32]{0,2,1:T(8,128)}), f32[192,64,32]{0,2,1:T(8,128)}, u32[]{:S(2)}, u32[]{:S(2)}) async-start(f32[192,64,32]{0,2,1:T(8,128)} %bitcast.104), calls=%async_computation.5 | async-start | bytes 4194304 | tf_op jit(solution)/shard_map/all_to_all | solution.py:236
  256.9 17.9 %copy-start.1 = (bf16[1,48,128,128]{3,2,1,0:T(8,128)(2,1)S(1)}, bf16[1,48,128,128]{3,2,1,0:T(8,128)(2,1)}, u32[]{:S(2)}) copy-start(bf16[1,48,128,128]{3,2,1,0:T(8,128)(2,1)} %param.10) | copy-start | bytes 4718596
Sparse Core Ops, SparseCore 0:
  9.8 32.8 all-gather.2
  44.6 29.1 all-gather.4

commit v2 on v0

v2 whole, which is shorter than its diff:
```python
import functools

import jax
import jax.numpy as jnp
from jax import lax
from jax.experimental import pallas as pl
from jax.experimental.pallas import tpu as pltpu
from jax.sharding import PartitionSpec as P

NX, NY, NZ, NC = 4, 4, 8, 2
NODES = NX * NZ * NC
GROUP = NZ * NC
X_ORDER = (2, 1, 3, 0)
MESH = pl.DeviceIdType.MESH
F32 = jnp.float32
BF16 = jnp.bfloat16
CONTRACT_FIRST = (((0,), (0,)), ((), ()))
CONTRACT_LAST = (((1,), (1,)), ((), ()))


def node_of(x, z, c):
    return (x * NZ + z) * NC + c


def remote(src, dst, send, recv, device):
    return pltpu.make_async_remote_copy(
        src_ref=src, dst_ref=dst, send_sem=send, recv_sem=recv, device_id=device, device_id_type=MESH
    )


def dot(a, b):
    return jnp.dot(a, b, preferred_element_type=F32)


def dot_last(a, b):
    return lax.dot_general(a, b, CONTRACT_LAST, preferred_element_type=F32)


def exchange_quarters(pieces):
    quarter = pieces[0].shape[1] // 4
    lane_quarter = lax.broadcasted_iota(jnp.int32, pieces[0].shape, 1) // quarter
    result = []
    for b in range(4):
        moved = pieces[b]
        for a in range(4):
            if a != b:
                rolled = pltpu.roll(pieces[a], ((a - b) % 4) * quarter, 1)
                moved = jnp.where(lane_quarter == a, rolled, moved)
        result.append(moved)
    return result


def layer_kernel(
    scale,
    table, picks, feat_hbm, tiles_hbm, wn_hbm, ws_hbm, cot_hbm,
    hidden_hbm, gfeat_ref, total_ref,
    feat, tiles, cot, weights, onehot, msg_out, msg_in, ext, running, agg_out, cols, pre, gate, hidden,
    back_out, back_in, own_term, other_term, core_in, x_out, x_in, y_out, y_in, z_out, z_in, z_sum,
    strip, rows, other, blocks, spread, acc,
    ret_out, ret_in,
    load_sem, halo_send, halo_recv, self_send, self_recv, w_send, w_recv, wf_send, wf_recv, wc_send, wc_recv,
    agg_send, agg_recv, ba_send, ba_recv, bs_send, bs_recv, c_send, c_recv, x_send, x_recv, y_send, y_recv,
    z_send, z_recv, zg_send, zg_recv, xg_send, xg_recv, cg_send, cg_recv, ret_send, ret_recv,
):
    n = lax.axis_index("node")
    y = lax.axis_index("feat")
    x, z, c = lax.div(n, GROUP), lax.rem(lax.div(n, NC), NZ), lax.rem(n, NC)
    partner = {"node": node_of(x, z, 1 - c)}
    y_of = lambda d: lax.rem(y + d, NY)
    x_of = lambda d: lax.rem(x + d, NX)
    z_of = lambda d: lax.rem(z + d, NZ)
    c_of = lambda d: lax.rem(c + d, NC)
    y_peer = lambda d: {"feat": y_of(d)}
    x_peer = lambda d: {"node": node_of(x_of(d), z, c)}
    z_peer = lambda d: {"node": node_of(x, z_of(d), c)}
    width, own_rows = feat.shape
    share = own_rows // NY
    side = tiles.shape[1]
    n_tiles = tiles.shape[0]
    own_blocks = own_rows // side
    lanes = GROUP * 32
    hid = gate.shape[1]
    xr, zc = width // NX, hid // NZ
    offsets = [(dx, dz, dc) for dx in X_ORDER for dz in range(NZ) for dc in range(NC) if dx or dz or dc]

    barrier = pltpu.get_barrier_semaphore()
    for dx, dz, dc in offsets:
        pl.semaphore_signal(
            barrier, inc=1, device_id={"node": node_of(x_of(dx), z_of(dz), c_of(dc))}, device_id_type=MESH
        )
    for d in range(1, NY):
        pl.semaphore_signal(barrier, inc=1, device_id=y_peer(d), device_id_type=MESH)

    loads = [
        pltpu.make_async_copy(feat_hbm, feat, load_sem.at[0]),
        pltpu.make_async_copy(wn_hbm, weights.at[0, y], load_sem.at[1]),
        pltpu.make_async_copy(ws_hbm, weights.at[1, y], load_sem.at[2]),
        pltpu.make_async_copy(tiles_hbm, tiles, load_sem.at[3]),
        pltpu.make_async_copy(cot_hbm, cot, load_sem.at[4]),
    ]
    for load in loads:
        load.start()
    loads[0].wait()
    msg_in[n] = jnp.zeros(msg_in.shape[1:], BF16)

    def pick(dx):
        part = x_of(dx)
        wanted = picks[part]
        ids = lax.broadcasted_iota(jnp.int32, (own_rows, lanes), 0)
        onehot[part] = jnp.where(ids == wanted, 1.0, 0.0).astype(BF16)
        picked = dot(feat[...], onehot[part])
        for b in range(lanes // side):
            block = picked[:, b * side:(b + 1) * side]
            height = width // 4
            moved = exchange_quarters([block[a * height:(a + 1) * height] for a in range(4)])
            for p in range(4):
                msg_out[part * GROUP + b * 4 + p] = moved[p].astype(BF16)

    def halo_copies(dx, out, into, send, recv):
        result = []
        for dz in range(NZ):
            for dc in range(NC):
                if dx or dz or dc:
                    o = (dx * NZ + dz) * NC + dc
                    peer = node_of(x_of(dx), z_of(dz), c_of(dc))
                    result.append(remote(out.at[peer], into.at[n], send.at[o], recv.at[o], {"node": peer}))
        return result

    def halo_waits(dx, out, into, send, recv):
        for dz in range(NZ):
            for dc in range(NC):
                if dx or dz or dc:
                    o = (dx * NZ + dz) * NC + dc
                    src = node_of(x_of(NX - dx), z_of(NZ - dz), c_of(NC - dc))
                    remote(out.at[src], into.at[src], send.at[o], recv.at[o], {"node": src}).wait_recv()

    pick(X_ORDER[0])
    pl.semaphore_wait(barrier, len(offsets) + NY - 1)
    halo = halo_copies(X_ORDER[0], msg_out, msg_in, halo_send, halo_recv)
    for cp in halo:
        cp.start()
    loads[1].wait()
    loads[2].wait()
    w_right = remote(weights.at[c, y], weights.at[c, y], w_send.at[0], w_recv.at[0], y_peer(1))
    w_left = remote(weights.at[c, y], weights.at[c, y], w_send.at[1], w_recv.at[1], y_peer(NY - 1))
    w_right.start()
    w_left.start()
    selfs = []
    for d in range(1, NY):
        q = y_of(d)
        cp = remote(
            feat_hbm.at[:, pl.ds(pl.multiple_of(q * share, share), share)], cols.at[1, y],
            self_send.at[d - 1], self_recv.at[d - 1], y_peer(d),
        )
        cp.start()
        selfs.append(cp)
    cols[1, y] = feat[:, pl.ds(pl.multiple_of(y * share, share), share)]
    for dx in X_ORDER[1:]:
        pick(dx)
        more = halo_copies(dx, msg_out, msg_in, halo_send, halo_recv)
        for cp in more:
            cp.start()
        halo = halo + more

    half = width // 2
    low, high = pl.ds(0, half), pl.ds(half, half)
    left_id, right_id, far_id = y_of(NY - 1), y_of(1), y_of(2)
    w_right.wait_recv()
    w_far_right = remote(
        weights.at[c, left_id, low], weights.at[c, left_id, low], wf_send.at[0], wf_recv.at[0], y_peer(1)
    )
    w_far_right.start()
    w_left.wait_recv()
    w_far_left = remote(
        weights.at[c, right_id, high], weights.at[c, right_id, high], wf_send.at[1], wf_recv.at[1], y_peer(NY - 1)
    )
    w_far_left.start()
    w_core = []
    for i, q in enumerate((left_id, right_id, far_id)):
        if i == 2:
            w_far_right.wait_recv()
            w_far_left.wait_recv()
        cp = remote(weights.at[c, q], weights.at[c, q], wc_send.at[i], wc_recv.at[i], partner)
        cp.start()
        w_core.append(cp)

    for b in range(own_blocks):
        ext[b] = feat[:, b * side:(b + 1) * side]
    loads[3].wait()
    height = width // 4

    def unpack(source, first):
        moved = exchange_quarters([source[first + p].astype(F32) for p in range(4)])
        return jnp.concatenate([piece.astype(BF16) for piece in moved], axis=0)

    for dx in X_ORDER:
        halo_waits(dx, msg_out, msg_in, halo_send, halo_recv)
        part = x_of(NX - dx)
        for b in range(GROUP // 4):
            ext[own_blocks + part * (GROUP // 4) + b] = unpack(msg_in, part * GROUP + b * 4)

    unroll = 4

    def aggregate(i, total):
        for u in range(unroll):
            s = i * unroll + u
            total = total * table[2, s].astype(F32) + dot_last(ext[table[1, s]], tiles[table[0, s]])
            running[s] = total.astype(BF16)
        return total

    lax.fori_loop(0, n_tiles // unroll, aggregate, jnp.zeros((width, side), F32))
    per = own_blocks // NY
    for r in range(own_blocks):
        agg_out[r // per, :, (r % per) * side:(r % per + 1) * side] = running[table[3, r]]
    aggs = []
    for d in range(1, NY):
        cp = remote(agg_out.at[y_of(d)], cols.at[0, y], agg_send.at[d - 1], agg_recv.at[d - 1], y_peer(d))
        cp.start()
        aggs.append(cp)
    cols[0, y] = agg_out[y]

    for cp in selfs:
        cp.wait_recv()
    for cp in w_core:
        cp.wait_recv()
    strips = 4
    wide = hid // strips

    def self_part(i, carry):
        at = pl.ds(pl.multiple_of(i * wide, wide), wide)
        left = cols[1].reshape(NY * width, share)
        right = weights[1, :, :, at].reshape(NY * width, wide)
        pre[:, at] = lax.dot_general(left, right, CONTRACT_FIRST, preferred_element_type=F32)
        return carry

    lax.fori_loop(0, strips, self_part, 0)
    loads[4].wait()
    for cp in aggs:
        cp.wait_recv()

    def neigh_part(i, carry):
        at = pl.ds(pl.multiple_of(i * wide, wide), wide)
        left = cols[0].reshape(NY * width, share)
        right = weights[0, :, :, at].reshape(NY * width, wide)
        value = pre[:, at] + lax.dot_general(left, right, CONTRACT_FIRST, preferred_element_type=F32)
        sig = jax.nn.sigmoid(value)
        hidden[:, at] = (value * sig).astype(BF16)
        gate[:, at] = (cot[:, at].astype(F32) * sig * (1.0 + value * (1.0 - sig))).astype(BF16)
        return carry

    lax.fori_loop(0, strips, neigh_part, 0)
    store_hidden = pltpu.make_async_copy(hidden, hidden_hbm, load_sem.at[5])
    store_hidden.start()

    backs = []
    for d in range(1, NY):
        q = y_of(d)
        back_out[0, q] = dot_last(weights[0, q], gate[...]).astype(BF16)
        cp = remote(back_out.at[0, q], back_in.at[0, y], ba_send.at[d - 1], ba_recv.at[d - 1], y_peer(d))
        cp.start()
        backs.append(cp)
    back_in[0, y] = dot_last(weights[0, y], gate[...]).astype(BF16)

    swaps = []
    for q in range(NY):
        other_term[q] = dot(cols[1 - c, q], gate[...]).astype(BF16)
        cp = remote(other_term.at[q], core_in.at[q], c_send.at[q], c_recv.at[q], partner)
        cp.start()
        swaps.append(cp)
    for q in range(NY):
        own_term[q] = dot(cols[c, q], gate[...])
    back_selfs = []
    for d in range(1, NY):
        q = y_of(d)
        back_out[1, q] = dot_last(weights[1, q], gate[...]).astype(BF16)
        cp = remote(back_out.at[1, q], back_in.at[1, y], bs_send.at[d - 1], bs_recv.at[d - 1], y_peer(d))
        cp.start()
        back_selfs.append(cp)
    back_in[1, y] = dot_last(weights[1, y], gate[...]).astype(BF16)

    for q in range(NY):
        swaps[q].wait_recv()
        for a in range(NX):
            at = slice(a * xr, (a + 1) * xr)
            both = own_term[q, at] + core_in[q, at].astype(F32)
            own_term[q, at] = both
            x_out[a, q] = both.astype(BF16)
    xs = []
    for d in range(1, NX):
        cp = remote(x_out.at[x_of(d)], x_in.at[d - 1], x_send.at[d - 1], x_recv.at[d - 1], x_peer(d))
        cp.start()
        xs.append(cp)

    for cp in backs:
        cp.wait_recv()
    for r in range(own_blocks):
        blocks[r] = back_in[0, r // per, :, (r % per) * side:(r % per + 1) * side]

    def spread_back(i, total):
        for u in range(unroll):
            s = i * unroll + u
            total = total * table[6, s].astype(F32) + dot(blocks[table[5, s]], tiles[table[4, s]])
            spread[s] = total
        return total

    lax.fori_loop(0, n_tiles // unroll, spread_back, jnp.zeros((width, side), F32))
    returns = []
    for dx in X_ORDER:
        part = x_of(dx)
        for b in range(GROUP // 4):
            col = own_blocks + part * (GROUP // 4) + b
            block = spread[table[7, col]] * table[8, col].astype(F32)
            moved = exchange_quarters([block[a * height:(a + 1) * height] for a in range(4)])
            for p in range(4):
                ret_out[part * GROUP + b * 4 + p] = moved[p].astype(BF16)
        more = halo_copies(dx, ret_out, ret_in, ret_send, ret_recv)
        for cp in more:
            cp.start()
        returns = returns + more
    ret_in[n] = jnp.zeros(ret_in.shape[1:], BF16)

    for cp in xs:
        cp.wait_recv()
    mine = own_term[:, pl.ds(pl.multiple_of(x * xr, xr), xr), :]
    for d in range(1, NX):
        mine = mine + x_in[d - 1].astype(F32)
    for q in range(NY):
        y_out[q] = mine[q].astype(BF16)
    ys = []
    for d in range(1, NY):
        cp = remote(y_out.at[y_of(d)], y_in.at[d - 1], y_send.at[d - 1], y_recv.at[d - 1], y_peer(d))
        cp.start()
        ys.append(cp)

    for cp in back_selfs:
        cp.wait_recv()
    for b in range(own_blocks):
        at = slice(b * side, (b + 1) * side)
        inner = slice((b % per) * side, (b % per + 1) * side)
        acc[:, at] = spread[table[7, b]] * table[8, b].astype(F32) + back_in[1, b // per, :, inner].astype(F32)

    for cp in ys:
        cp.wait_recv()
    mine = y_out[y].astype(F32)
    for d in range(1, NY):
        mine = mine + y_in[d - 1].astype(F32)
    for q in range(NZ):
        z_out[q] = mine[:, q * zc:(q + 1) * zc].astype(BF16)
    zs = []
    for d in range(1, NZ):
        cp = remote(z_out.at[z_of(d)], z_in.at[d - 1], z_send.at[d - 1], z_recv.at[d - 1], z_peer(d))
        cp.start()
        zs.append(cp)
    for cp in zs:
        cp.wait_recv()
    mine = z_out[z].astype(F32)
    for d in range(1, NZ):
        mine = mine + z_in[d - 1].astype(F32)
    z_sum[...] = mine.astype(BF16)
    zgs = []
    for d in range(1, NZ):
        cp = remote(z_sum, strip.at[z], zg_send.at[d - 1], zg_recv.at[d - 1], z_peer(d))
        cp.start()
        zgs.append(cp)
    strip[z] = z_sum[...]
    for cp in zgs:
        cp.wait_recv()
    xgs = []
    for d in range(1, NX):
        cp = remote(strip, rows.at[x], xg_send.at[d - 1], xg_recv.at[d - 1], x_peer(d))
        cp.start()
        xgs.append(cp)
    rows[x] = strip[...]

    def scatter(dx):
        halo_waits(dx, ret_out, ret_in, ret_send, ret_recv)
        part = x_of(NX - dx)
        came = jnp.concatenate(
            [unpack(ret_in, part * GROUP + b * 4) for b in range(GROUP // 4)], axis=1
        )
        acc[...] += dot_last(came, onehot[part])

    scatter(X_ORDER[0])
    for cp in xgs:
        cp.wait_recv()
    last = remote(rows, other, cg_send.at[0], cg_recv.at[0], partner)
    last.start()
    for dx in X_ORDER[1:]:
        scatter(dx)
    gfeat_ref[...] = acc[...].astype(BF16)
    last.wait_recv()
    for a in range(NX):
        for b in range(NZ):
            ra, cb = slice(a * xr, (a + 1) * xr), slice(b * zc, (b + 1) * zc)
            total_ref[c, ra, cb] = rows[a, b].astype(F32) * scale
            total_ref[1 - c, ra, cb] = other[a, b].astype(F32) * scale
    store_hidden.wait()
    for cp in (
        halo + selfs + [w_right, w_left, w_far_right, w_far_left] + w_core + aggs + backs + swaps + back_selfs
        + xs + returns + ys + zs + zgs + xgs + [last]
    ):
        cp.wait_send()


def layer(table, picks, feat, tiles, wn, ws, cot, scale):
    width, own_rows = feat.shape
    n_tiles, side, _ = tiles.shape
    share, hid = cot.shape
    xr, zc = width // NX, hid // NZ
    own_blocks = own_rows // side
    lanes = own_rows // NX
    height = width // 4
    vmem = pltpu.VMEM
    dma = lambda k: pltpu.SemaphoreType.DMA((k,))
    any_space = pl.BlockSpec(memory_space=pl.ANY)
    in_vmem = pl.BlockSpec(memory_space=pltpu.VMEM)
    return pl.pallas_call(
        functools.partial(layer_kernel, scale),
        out_shape=(
            jax.ShapeDtypeStruct((share, hid), BF16),
            jax.ShapeDtypeStruct((width, own_rows), BF16),
            jax.ShapeDtypeStruct((NC, width, hid), F32),
        ),
        in_specs=[pl.BlockSpec(memory_space=pltpu.SMEM), in_vmem] + [any_space] * 5,
        out_specs=(any_space, in_vmem, in_vmem),
        scratch_shapes=[
            vmem((width, own_rows), BF16),
            vmem((n_tiles, side, side), BF16),
            vmem((share, hid), BF16),
            vmem((2, NY, width, hid), BF16),
            vmem((NX, own_rows, lanes), BF16),
            vmem((NODES, height, side), BF16),
            vmem((NODES, height, side), BF16),
            vmem((2 * own_blocks, width, side), BF16),
            vmem((n_tiles, width, side), BF16),
            vmem((NY, width, share), BF16),
            vmem((2, NY, width, share), BF16),
            vmem((share, hid), F32),
            vmem((share, hid), BF16),
            vmem((share, hid), BF16),
            vmem((2, NY, width, share), BF16),
            vmem((2, NY, width, share), BF16),
            vmem((NY, width, hid), F32),
            vmem((NY, width, hid), BF16),
            vmem((NY, width, hid), BF16),
            vmem((NX, NY, xr, hid), BF16),
            vmem((NX - 1, NY, xr, hid), BF16),
            vmem((NY, xr, hid), BF16),
            vmem((NY - 1, xr, hid), BF16),
            vmem((NZ, xr, zc), BF16),
            vmem((NZ - 1, xr, zc), BF16),
            vmem((xr, zc), BF16),
            vmem((NZ, xr, zc), BF16),
            vmem((NX, NZ, xr, zc), BF16),
            vmem((NX, NZ, xr, zc), BF16),
            vmem((own_blocks, width, side), BF16),
            vmem((n_tiles, width, side), F32),
            vmem((width, own_rows), F32),
            vmem((NODES, height, side), BF16),
            vmem((NODES, height, side), BF16),
            dma(6), dma(NODES), dma(NODES), dma(3), dma(3), dma(2), dma(2), dma(2), dma(2), dma(3), dma(3),
            dma(3), dma(3), dma(3), dma(3), dma(3), dma(3), dma(4), dma(4), dma(3), dma(3), dma(3), dma(3),
            dma(7), dma(7), dma(7), dma(7), dma(3), dma(3), dma(1), dma(1), dma(NODES), dma(NODES),
        ],
        compiler_params=pltpu.CompilerParams(
            collective_id=0, has_side_effects=True, vmem_limit_bytes=60 << 20
        ),
        name="sage_layer",
    )(table, picks, feat, tiles, wn, ws, cot)


def tile_order(row_ids, col_ids, col_blocks):
    count = row_ids.shape[0]
    keys = jnp.stack([row_ids, col_ids])
    place = lax.broadcasted_iota(jnp.int32, (count,), 0)
    before = (keys[:, None, :] < keys[:, :, None]) | (
        (keys[:, None, :] == keys[:, :, None]) & (place[None, None, :] < place[None, :, None])
    )
    rank = jnp.sum(before.astype(jnp.int32), axis=2)
    chosen = (rank[:, None, :] == place[None, :, None]).astype(jnp.int32)
    order = jnp.sum(chosen * place[None, None, :], axis=2)
    own = jnp.sum(chosen * keys[:, None, :], axis=2)
    across = jnp.sum(chosen * keys[::-1][:, None, :], axis=2)
    earlier = jnp.concatenate([jnp.full((2, 1), -1, jnp.int32), own[:, :-1]], axis=1)
    keep = (own == earlier).astype(jnp.int32)
    ids = lax.broadcasted_iota(jnp.int32, (count,), 0)
    upto = jnp.sum((keys[:, None, :] <= ids[None, :, None]).astype(jnp.int32), axis=2)
    has = jnp.sum((keys[:, None, :] == ids[None, :, None]).astype(jnp.int32), axis=2) > 0
    last = jnp.maximum(upto - 1, 0)
    return jnp.stack(
        [order[0], across[0], keep[0], last[0], order[1], across[1], keep[1], last[1], has[1].astype(jnp.int32)]
    )


def per_device(
    features, tiles, tile_rows, tile_cols, send_rows, send_count, w_neigh, w_self, cotangent
):
    own_rows = features.shape[2]
    parts, slots = send_rows.shape[1:]
    live = lax.broadcasted_iota(jnp.int32, (parts, slots), 1) < send_count[0][:, None]
    picks = jnp.where(live, send_rows[0], -1).reshape(NX, 1, parts * slots // NX)
    col_blocks = (own_rows + parts * slots) // tiles.shape[2]
    table = tile_order(tile_rows[0], tile_cols[0], col_blocks)
    grad_scale = float(own_rows * lax.axis_size("node")) ** (-0.5)
    hidden, grad_features, totals = layer(
        table, picks, features[0], tiles[0], w_neigh, w_self, cotangent[0], grad_scale
    )
    return hidden[None], grad_features[None], totals[0], totals[1]


def solution(mesh):
    placed = (
        P("node", "feat", None),
        P("node", None, None, None),
        P("node", None),
        P("node", None),
        P("node", None, None),
        P("node", None),
        P("feat", None),
        P("feat", None),
        P("node", "feat", None),
    )
    return jax.shard_map(
        per_device,
        mesh=mesh,
        in_specs=placed,
        out_specs=(
            P("node", "feat", None),
            P("node", "feat", None),
            P("feat", None),
            P("feat", None),
        ),
        check_vma=False,
    )
```

time: 421 us -> 129 us (0.31)
  waiting for transfers between devices: 253 us -> 0 us
  Pallas kernels: 0 us -> 116 us
  starting transfers between devices: 38.7 us -> 0 us
  matrix products: 37 us -> 0 us
  local copies, waits for them, and re-layouts: 41.9 us -> 8.15 us
  other arithmetic: 35 us -> 3.15 us
  between operations: 14 us -> 0.7 us
    psum x1 -> x0, waiting for transfers between devices: 143 us -> none  [per_device(): total_neigh, total_self = lax.psum((share_neigh, share_self), 'node')]
    pallas_call x0 -> x1, Pallas kernels: none -> 116 us  [layer(): pl.pallas_call(functools.partial(layer_kernel, scale), out_shape=(jax.Sha...]
    all_to_all x6 -> x0, waiting for transfers between devices: 85.7 us -> none  [the longest x1 29 us: per_device(): lax.all_to_all(outgoing, 'node', split_axis=1, concat_axis=1, tiled=True)]
    all_to_all x6 -> x0, starting transfers between devices: 38 us -> none  [the longest x1 13 us: per_device(): lax.all_to_all(picked, 'node', split_axis=1, concat_axis=1, tiled=True)]
    dot_general x10 -> x0, matrix products: 37 us -> none  [the longest x1 6.55 us: per_device(): jnp.einsum('fkj,kc->fcj', spread, col_onehot, precision=lax.Precision.HIG...]
    reduce_scatter x2 -> x0, waiting for transfers between devices: 22.7 us -> none  [the longest x1 22.7 us: per_device(): lax.psum_scatter(term_self, 'feat', scatter_dimension=0, tiled=True)]
    scatter-add x1 -> x0, other arithmetic: 14.9 us -> none  [per_device(): grad_cols.at[:, targets.reshape(-1)]]
    gather x3 -> x0, local copies, waits for them, and re-layouts: 13.8 us -> none  [the longest x1 9.06 us: per_device(): jnp.take(own_cols, targets.reshape(-1), axis=1)]
  transfers between devices with their start and end apart: 11 -> 0, of which waited for: 7 -> 0; matrix products, arithmetic and copies ran while one was open for 24% -> 0% of each run, Pallas kernels for 0% -> 0%
where the time goes in v2:
time: 129 us; the launch traced here: 128 us
  Pallas kernels  116 us (90%)
  local copies, waits for them, and re-layouts  8.15 us (6%)
  other arithmetic  3.15 us (2%)
    pallas_call x1, Pallas kernels, layer(): pl.pallas_call(functools.partial(layer_kernel, scale), out_shape=(jax.Sha...  116 us
    unnamed x8, local copies, waits for them, and re-layouts  3.7 us
    squeeze x1, local copies, waits for them, and re-layouts, per_device(): return (hidden[None], grad_features[None], totals[0], totals[1])  2.77 us

profile of v2, /device:TPU:1, one launch (start us, length us, event | category | flops | bytes accessed | tf_op | source)
XLA Modules:
  0.0 128.3 jit_solution(17760933889858224802)
XLA Ops:
  0.6 0.5 broadcast.65
  1.1 1.3 %reduce.3 = s32[64]{0:T(128)S(1)} reduce(s32[1,64]{1,0:T(1,128)} %param.14, s32[]{:T(128)} %broadcast.65), dimensions={0}, to_apply=%param.14.reduce_sub_computation.3 | reduce | bytes 516 | tf_op args[5]
  2.5 0.7 pad_add_fusion
  3.2 0.1 lt.56
  3.3 0.2 convert_reduce_fusion.2
  3.5 0.3 convert_reduce_fusion
  3.7 0.1 compare_convert_fusion
  3.8 1.2 stack.8.table
  5.1 0.1 iota.33
  5.1 0.1 lt.57
  5.2 0.1 lt.58
  5.3 0.8 copy.16
  6.1 0.1 squeeze.25
  6.2 0.6 compare_select_fusion.picks
  6.8 116.3 %sage_layer.1 = (bf16[512,1024]{1,0:T(8,128)(2,1)}, bf16[192,2048]{1,0:T(8,128)(2,1)}, f32[2,192,1024]{2,1,0:T(8,128)}) custom-call(s32[9,48]{1,0:T(8,128)} %stack.8.table, s32[4,1,512]{2,1,0:T(1,128)} %compare_select_fusion.picks, bf16[192,2048]{1,0:T(8,128)(2,1)} %bitcast.13, bf16[48,128,128]{2,1,0:T(8,128)(2,1)} %bitcast.10, bf16[192,1024]{1,0:T(8,128)(2,1)} %wn_hbm.1, ...), custom_call_target="tpu_custom_call" | custom-call | tf_op jit(solution)/shard_map/sage_layer/pallas_call | solution.py:417
  123.2 0.0 copy-start
  123.2 2.8 %slice_bitcast_fusion = (f32[192,1024]{1,0:T(8,128)}, f32[192,1024]{1,0:T(8,128)}) fusion(f32[2,192,1024]{2,1,0:T(8,128)} %get-tuple-element.9), kind=kLoop, calls=%fused_computation | loop fusion | bytes 3145728 | tf_op jit(solution)/shard_map/squeeze | solution.py:508
  126.0 0.0 copy-start.1
  126.0 0.0 copy-done
  126.0 1.0 copy.20
  126.9 0.5 copy-done.1
  127.5 0.9 copy.21
  (8 shorter events, 0.1 us)
Async XLA Ops:
  123.2 2.8 %copy-start = (bf16[512,1024]{1,0:T(8,128)(2,1)S(1)}, bf16[512,1024]{1,0:T(8,128)(2,1)}, u32[]{:S(2)}) copy-start(bf16[512,1024]{1,0:T(8,128)(2,1)} %get-tuple-element.7) | copy-start | bytes 3145732
  126.0 1.5 %copy-start.1 = (bf16[192,2048]{1,0:T(8,128)(2,1)S(1)}, bf16[192,2048]{1,0:T(8,128)(2,1)}, u32[]{:S(2)}) copy-start(bf16[192,2048]{1,0:T(8,128)(2,1)} %get-tuple-element.8) | copy-start | bytes 2359300

commit v3 on v2

v3 whole, which is shorter than its diff:
```python
import functools

import jax
import jax.numpy as jnp
from jax import lax
from jax.experimental import pallas as pl
from jax.experimental.pallas import tpu as pltpu
from jax.sharding import PartitionSpec as P

NX, NY, NZ, NC = 4, 4, 8, 2
NODES = NX * NZ * NC
GROUP = NZ * NC
X_ORDER = (2, 1, 3, 0)
MESH = pl.DeviceIdType.MESH
F32 = jnp.float32
BF16 = jnp.bfloat16
CONTRACT_FIRST = (((0,), (0,)), ((), ()))
CONTRACT_LAST = (((1,), (1,)), ((), ()))


def node_of(x, z, c):
    return (x * NZ + z) * NC + c


def remote(src, dst, send, recv, device):
    return pltpu.make_async_remote_copy(
        src_ref=src, dst_ref=dst, send_sem=send, recv_sem=recv, device_id=device, device_id_type=MESH
    )


def dot(a, b):
    return jnp.dot(a, b, preferred_element_type=F32)


def dot_last(a, b):
    return lax.dot_general(a, b, CONTRACT_LAST, preferred_element_type=F32)


def exchange_quarters(pieces):
    quarter = pieces[0].shape[1] // 4
    lane_quarter = lax.broadcasted_iota(jnp.int32, pieces[0].shape, 1) // quarter
    result = []
    for b in range(4):
        moved = pieces[b]
        for a in range(4):
            if a != b:
                rolled = pltpu.roll(pieces[a], ((a - b) % 4) * quarter, 1)
                moved = jnp.where(lane_quarter == a, rolled, moved)
        result.append(moved)
    return result


def tile_table(row_ref, col_ref, out_ref):
    count = row_ref.shape[1]
    upright = lax.broadcasted_iota(jnp.int32, (count, count), 0)
    across = lax.broadcasted_iota(jnp.int32, (count, count), 1)
    stand = lambda line: jnp.sum(jnp.where(upright == across, line, 0), axis=1, keepdims=True)
    column = lambda mask, value: jnp.sum(jnp.where(mask, value, 0), axis=0, keepdims=True)
    keys = row_ref[...], col_ref[...]
    stood = [stand(line) for line in keys]
    for t in range(2):
        line, post = keys[t], stood[t]
        before = (line < post) | ((line == post) & (across < upright))
        rank = jnp.sum(before.astype(jnp.int32), axis=1, keepdims=True)
        chosen = rank == across
        own = column(chosen, post)
        previous = column(rank == across - 1, post)
        results = (
            column(chosen, upright),
            column(chosen, stood[1 - t]),
            jnp.where((own == previous) & (across[:1] > 0), 1, 0),
            jnp.maximum(column(post <= across, 1) - 1, 0),
            jnp.minimum(column(post == across, 1), 1),
        )
        for i, result in enumerate(results):
            out_ref[t * 5 + i, :, pl.ds(0, count)] = result


def layer_kernel(
    scale,
    row_ref, col_ref, picks, feat_hbm, tiles_hbm, wn_hbm, ws_hbm, cot_hbm,
    hidden_hbm, gfeat_ref, total_neigh, total_self,
    feat, tiles, cot, weights, onehot, msg_out, msg_in, ext, running, agg_out, cols, pre, gate, hidden,
    back_out, back_in, own_term, other_term, core_in, x_out, x_in, y_out, y_in, z_out, z_in, z_sum,
    strip, rows, other, blocks, spread, acc,
    ret_out, ret_in, table_rows, table,
    load_sem, halo_send, halo_recv, self_send, self_recv, w_send, w_recv, wf_send, wf_recv, wc_send, wc_recv,
    agg_send, agg_recv, ba_send, ba_recv, bs_send, bs_recv, c_send, c_recv, x_send, x_recv, y_send, y_recv,
    z_send, z_recv, zg_send, zg_recv, xg_send, xg_recv, cg_send, cg_recv, ret_send, ret_recv,
):
    n = lax.axis_index("node")
    y = lax.axis_index("feat")
    x, z, c = lax.div(n, GROUP), lax.rem(lax.div(n, NC), NZ), lax.rem(n, NC)
    partner = {"node": node_of(x, z, 1 - c)}
    y_of = lambda d: lax.rem(y + d, NY)
    x_of = lambda d: lax.rem(x + d, NX)
    z_of = lambda d: lax.rem(z + d, NZ)
    c_of = lambda d: lax.rem(c + d, NC)
    y_peer = lambda d: {"feat": y_of(d)}
    x_peer = lambda d: {"node": node_of(x_of(d), z, c)}
    z_peer = lambda d: {"node": node_of(x, z_of(d), c)}
    width, own_rows = feat.shape
    share = own_rows // NY
    side = tiles.shape[1]
    n_tiles = tiles.shape[0]
    own_blocks = own_rows // side
    lanes = GROUP * 32
    hid = gate.shape[1]
    xr, zc = width // NX, hid // NZ
    offsets = [(dx, dz, dc) for dx in X_ORDER for dz in range(NZ) for dc in range(NC) if dx or dz or dc]

    started, due = [], {}

    def start(cp):
        cp.start()
        started.append(cp)
        due[id(cp)] = cp.wait_recv
        return cp

    def arrive(copies):
        for cp in copies:
            due.pop(id(cp))()

    barrier = pltpu.get_barrier_semaphore()
    for dx, dz, dc in offsets:
        pl.semaphore_signal(
            barrier, inc=1, device_id={"node": node_of(x_of(dx), z_of(dz), c_of(dc))}, device_id_type=MESH
        )
    for d in range(1, NY):
        pl.semaphore_signal(barrier, inc=1, device_id=y_peer(d), device_id_type=MESH)

    loads = [
        pltpu.make_async_copy(feat_hbm, feat, load_sem.at[0]),
        pltpu.make_async_copy(wn_hbm, weights.at[0, y], load_sem.at[1]),
        pltpu.make_async_copy(ws_hbm, weights.at[1, y], load_sem.at[2]),
        pltpu.make_async_copy(tiles_hbm, tiles, load_sem.at[3]),
        pltpu.make_async_copy(cot_hbm, cot, load_sem.at[4]),
    ]
    for load in loads:
        load.start()
    loads[0].wait()
    msg_in[n] = jnp.zeros(msg_in.shape[1:], BF16)

    def pick(dx):
        part = x_of(dx)
        wanted = picks[part]
        ids = lax.broadcasted_iota(jnp.int32, (own_rows, lanes), 0)
        onehot[part] = jnp.where(ids == wanted, 1.0, 0.0).astype(BF16)
        picked = dot(feat[...], onehot[part])
        for b in range(lanes // side):
            block = picked[:, b * side:(b + 1) * side]
            height = width // 4
            moved = exchange_quarters([block[a * height:(a + 1) * height] for a in range(4)])
            for p in range(4):
                msg_out[part * GROUP + b * 4 + p] = moved[p].astype(BF16)

    def halo_start(dx, out, into, send, recv):
        for dz in range(NZ):
            for dc in range(NC):
                if dx or dz or dc:
                    o = (dx * NZ + dz) * NC + dc
                    peer = node_of(x_of(dx), z_of(dz), c_of(dc))
                    cp = remote(out.at[peer], into.at[n], send.at[o], recv.at[o], {"node": peer})
                    cp.start()
                    started.append(cp)
        due[id(into), dx] = functools.partial(halo_arrive, dx, out, into, send, recv)

    def halo_arrive(dx, out, into, send, recv):
        for dz in range(NZ):
            for dc in range(NC):
                if dx or dz or dc:
                    o = (dx * NZ + dz) * NC + dc
                    src = node_of(x_of(NX - dx), z_of(NZ - dz), c_of(NC - dc))
                    remote(out.at[src], into.at[src], send.at[o], recv.at[o], {"node": src}).wait_recv()

    pick(X_ORDER[0])
    pl.semaphore_wait(barrier, len(offsets) + NY - 1)
    halo_start(X_ORDER[0], msg_out, msg_in, halo_send, halo_recv)
    loads[1].wait()
    loads[2].wait()
    w_right = remote(weights.at[c, y], weights.at[c, y], w_send.at[0], w_recv.at[0], y_peer(1))
    w_left = remote(weights.at[c, y], weights.at[c, y], w_send.at[1], w_recv.at[1], y_peer(NY - 1))
    start(w_right)
    start(w_left)
    selfs = []
    for d in range(1, NY):
        q = y_of(d)
        cp = remote(
            feat_hbm.at[:, pl.ds(pl.multiple_of(q * share, share), share)], cols.at[1, y],
            self_send.at[d - 1], self_recv.at[d - 1], y_peer(d),
        )
        selfs.append(start(cp))
    cols[1, y] = feat[:, pl.ds(pl.multiple_of(y * share, share), share)]
    for dx in X_ORDER[1:]:
        pick(dx)
        halo_start(dx, msg_out, msg_in, halo_send, halo_recv)

    half = width // 2
    low, high = pl.ds(0, half), pl.ds(half, half)
    left_id, right_id, far_id = y_of(NY - 1), y_of(1), y_of(2)
    arrive([w_right])
    w_far_right = remote(
        weights.at[c, left_id, low], weights.at[c, left_id, low], wf_send.at[0], wf_recv.at[0], y_peer(1)
    )
    start(w_far_right)
    arrive([w_left])
    w_far_left = remote(
        weights.at[c, right_id, high], weights.at[c, right_id, high], wf_send.at[1], wf_recv.at[1], y_peer(NY - 1)
    )
    start(w_far_left)
    w_core = []
    for i, q in enumerate((left_id, right_id, far_id)):
        if i == 2:
            arrive([w_far_right])
            arrive([w_far_left])
        cp = remote(weights.at[c, q], weights.at[c, q], wc_send.at[i], wc_recv.at[i], partner)
        w_core.append(start(cp))

    tile_table(row_ref, col_ref, table_rows)
    table_copy = pltpu.make_async_copy(table_rows, table, load_sem.at[6])
    table_copy.start()
    for b in range(own_blocks):
        ext[b] = feat[:, b * side:(b + 1) * side]
    loads[3].wait()
    table_copy.wait()
    height = width // 4

    def unpack(source, first):
        moved = exchange_quarters([source[first + p].astype(F32) for p in range(4)])
        return jnp.concatenate([piece.astype(BF16) for piece in moved], axis=0)

    for dx in X_ORDER:
        due.pop((id(msg_in), dx))()
        part = x_of(NX - dx)
        for b in range(GROUP // 4):
            ext[own_blocks + part * (GROUP // 4) + b] = unpack(msg_in, part * GROUP + b * 4)

    unroll = 4

    def aggregate(i, total):
        for u in range(unroll):
            s = i * unroll + u
            total = total * table[2, 0, s].astype(F32) + dot_last(ext[table[1, 0, s]], tiles[table[0, 0, s]])
            running[s] = total.astype(BF16)
        return total

    lax.fori_loop(0, n_tiles // unroll, aggregate, jnp.zeros((width, side), F32))
    per = own_blocks // NY
    for r in range(own_blocks):
        agg_out[r // per, :, (r % per) * side:(r % per + 1) * side] = running[table[3, 0, r]]
    aggs = []
    for d in range(1, NY):
        cp = remote(agg_out.at[y_of(d)], cols.at[0, y], agg_send.at[d - 1], agg_recv.at[d - 1], y_peer(d))
        aggs.append(start(cp))
    cols[0, y] = agg_out[y]

    arrive(selfs)
    arrive(w_core)
    strips = 4
    wide = hid // strips

    def self_part(i, carry):
        at = pl.ds(pl.multiple_of(i * wide, wide), wide)
        left = cols[1].reshape(NY * width, share)
        right = weights[1, :, :, at].reshape(NY * width, wide)
        pre[:, at] = lax.dot_general(left, right, CONTRACT_FIRST, preferred_element_type=F32)
        return carry

    lax.fori_loop(0, strips, self_part, 0)
    loads[4].wait()
    arrive(aggs)

    def neigh_part(i, carry):
        at = pl.ds(pl.multiple_of(i * wide, wide), wide)
        left = cols[0].reshape(NY * width, share)
        right = weights[0, :, :, at].reshape(NY * width, wide)
        value = pre[:, at] + lax.dot_general(left, right, CONTRACT_FIRST, preferred_element_type=F32)
        sig = jax.nn.sigmoid(value)
        hidden[:, at] = (value * sig).astype(BF16)
        gate[:, at] = (cot[:, at].astype(F32) * sig * (1.0 + value * (1.0 - sig))).astype(BF16)
        return carry

    lax.fori_loop(0, strips, neigh_part, 0)
    store_hidden = pltpu.make_async_copy(hidden, hidden_hbm, load_sem.at[5])
    store_hidden.start()

    backs = []
    for d in range(1, NY):
        q = y_of(d)
        back_out[0, q] = dot_last(weights[0, q], gate[...]).astype(BF16)
        cp = remote(back_out.at[0, q], back_in.at[0, y], ba_send.at[d - 1], ba_recv.at[d - 1], y_peer(d))
        backs.append(start(cp))
    back_in[0, y] = dot_last(weights[0, y], gate[...]).astype(BF16)

    y_order = (1, 2, 3, 0)
    swaps, xs, ys = {}, {}, []
    for d in y_order:
        q = y_of(d)
        other_term[q] = dot(cols[1 - c, q], gate[...]).astype(BF16)
        swaps[d] = start(remote(other_term.at[q], core_in.at[q], c_send.at[d], c_recv.at[d], partner))
    for d in y_order:
        q = y_of(d)
        term = dot(cols[c, q], gate[...])
        arrive([swaps[d]])
        own_term[q] = term + core_in[q].astype(F32)
        xs[d] = []
        for e in range(1, NX):
            at = pl.ds(pl.multiple_of(x_of(e) * xr, xr), xr)
            x_out[e - 1, q] = own_term[q, at].astype(BF16)
            k = d * (NX - 1) + e - 1
            xs[d].append(
                start(remote(x_out.at[e - 1, q], x_in.at[e - 1, q], x_send.at[k], x_recv.at[k], x_peer(e)))
            )
    back_selfs = []
    for d in range(1, NY):
        q = y_of(d)
        back_out[1, q] = dot_last(weights[1, q], gate[...]).astype(BF16)
        cp = remote(back_out.at[1, q], back_in.at[1, y], bs_send.at[d - 1], bs_recv.at[d - 1], y_peer(d))
        back_selfs.append(start(cp))
    back_in[1, y] = dot_last(weights[1, y], gate[...]).astype(BF16)

    def sum_over_x(d):
        q = y_of(d)
        arrive(xs[d])
        mine = own_term[q, pl.ds(pl.multiple_of(x * xr, xr), xr)]
        for e in range(1, NX):
            mine = mine + x_in[e - 1, q].astype(F32)
        return mine

    def send_over_y(d):
        y_out[d - 1] = sum_over_x(d).astype(BF16)
        ys.append(start(remote(y_out.at[d - 1], y_in.at[d - 1], y_send.at[d - 1], y_recv.at[d - 1], y_peer(d))))

    arrive(backs)
    for r in range(own_blocks):
        blocks[r] = back_in[0, r // per, :, (r % per) * side:(r % per + 1) * side]

    def spread_back(i, total):
        for u in range(unroll):
            s = i * unroll + u
            total = total * table[7, 0, s].astype(F32) + dot(blocks[table[6, 0, s]], tiles[table[5, 0, s]])
            spread[s] = total
        return total

    lax.fori_loop(0, n_tiles // unroll, spread_back, jnp.zeros((width, side), F32))

    def send_back(dx):
        part = x_of(dx)
        for b in range(GROUP // 4):
            col = own_blocks + part * (GROUP // 4) + b
            block = spread[table[8, 0, col]] * table[9, 0, col].astype(F32)
            moved = exchange_quarters([block[a * height:(a + 1) * height] for a in range(4)])
            for p in range(4):
                ret_out[part * GROUP + b * 4 + p] = moved[p].astype(BF16)
        halo_start(dx, ret_out, ret_in, ret_send, ret_recv)

    def scatter(dx):
        due.pop((id(ret_in), dx))()
        part = x_of(NX - dx)
        came = jnp.concatenate(
            [unpack(ret_in, part * GROUP + b * 4) for b in range(GROUP // 4)], axis=1
        )
        acc[...] += dot_last(came, onehot[part])

    ret_in[n] = jnp.zeros(ret_in.shape[1:], BF16)
    send_back(X_ORDER[0])
    send_over_y(1)
    send_over_y(2)
    send_back(X_ORDER[1])
    send_over_y(3)
    mine = sum_over_x(0)
    arrive(ys)
    for d in range(1, NY):
        mine = mine + y_in[d - 1].astype(F32)
    for q in range(NZ):
        z_out[q] = mine[:, q * zc:(q + 1) * zc].astype(BF16)
    zs = []
    for d in range(1, NZ):
        cp = remote(z_out.at[z_of(d)], z_in.at[d - 1], z_send.at[d - 1], z_recv.at[d - 1], z_peer(d))
        zs.append(start(cp))
    send_back(X_ORDER[2])
    arrive(back_selfs)
    for b in range(own_blocks):
        at = slice(b * side, (b + 1) * side)
        inner = slice((b % per) * side, (b % per + 1) * side)
        acc[:, at] = spread[table[8, 0, b]] * table[9, 0, b].astype(F32) + back_in[1, b // per, :, inner].astype(F32)
    arrive(zs)
    mine = z_out[z].astype(F32)
    for d in range(1, NZ):
        mine = mine + z_in[d - 1].astype(F32)
    z_sum[...] = mine.astype(BF16)
    zgs = []
    for d in range(1, NZ):
        cp = remote(z_sum, strip.at[z], zg_send.at[d - 1], zg_recv.at[d - 1], z_peer(d))
        zgs.append(start(cp))
    strip[z] = z_sum[...]
    send_back(X_ORDER[3])
    scatter(X_ORDER[0])
    arrive(zgs)
    xgs = []
    for d in range(1, NX):
        cp = remote(strip, rows.at[x], xg_send.at[d - 1], xg_recv.at[d - 1], x_peer(d))
        xgs.append(start(cp))
    rows[x] = strip[...]
    scatter(X_ORDER[1])
    arrive(xgs)
    last = start(remote(rows, other, cg_send.at[0], cg_recv.at[0], partner))
    for dx in X_ORDER[2:]:
        scatter(dx)
    gfeat_ref[...] = acc[...].astype(BF16)
    arrive([last])
    for a in range(NX):
        for b in range(NZ):
            ra, cb = slice(a * xr, (a + 1) * xr), slice(b * zc, (b + 1) * zc)
            mine, theirs = rows[a, b].astype(F32) * scale, other[a, b].astype(F32) * scale
            total_neigh[ra, cb] = jnp.where(c == 0, mine, theirs)
            total_self[ra, cb] = jnp.where(c == 0, theirs, mine)
    store_hidden.wait()
    for cp in started:
        cp.wait_send()


def layer(row_ids, col_ids, picks, feat, tiles, wn, ws, cot, scale):
    width, own_rows = feat.shape
    n_tiles, side, _ = tiles.shape
    share, hid = cot.shape
    xr, zc = width // NX, hid // NZ
    own_blocks = own_rows // side
    lanes = own_rows // NX
    height = width // 4
    vmem = pltpu.VMEM
    dma = lambda k: pltpu.SemaphoreType.DMA((k,))
    any_space = pl.BlockSpec(memory_space=pl.ANY)
    in_vmem = pl.BlockSpec(memory_space=pltpu.VMEM)
    return pl.pallas_call(
        functools.partial(layer_kernel, scale),
        out_shape=(
            jax.ShapeDtypeStruct((share, hid), BF16),
            jax.ShapeDtypeStruct((width, own_rows), BF16),
            jax.ShapeDtypeStruct((width, hid), F32),
            jax.ShapeDtypeStruct((width, hid), F32),
        ),
        in_specs=[in_vmem] * 3 + [any_space] * 5,
        out_specs=(any_space, in_vmem, in_vmem, in_vmem),
        scratch_shapes=[
            vmem((width, own_rows), BF16),
            vmem((n_tiles, side, side), BF16),
            vmem((share, hid), BF16),
            vmem((2, NY, width, hid), BF16),
            vmem((NX, own_rows, lanes), BF16),
            vmem((NODES, height, side), BF16),
            vmem((NODES, height, side), BF16),
            vmem((2 * own_blocks, width, side), BF16),
            vmem((n_tiles, width, side), BF16),
            vmem((NY, width, share), BF16),
            vmem((2, NY, width, share), BF16),
            vmem((share, hid), F32),
            vmem((share, hid), BF16),
            vmem((share, hid), BF16),
            vmem((2, NY, width, share), BF16),
            vmem((2, NY, width, share), BF16),
            vmem((NY, width, hid), F32),
            vmem((NY, width, hid), BF16),
            vmem((NY, width, hid), BF16),
            vmem((NX - 1, NY, xr, hid), BF16),
            vmem((NX - 1, NY, xr, hid), BF16),
            vmem((NY - 1, xr, hid), BF16),
            vmem((NY - 1, xr, hid), BF16),
            vmem((NZ, xr, zc), BF16),
            vmem((NZ - 1, xr, zc), BF16),
            vmem((xr, zc), BF16),
            vmem((NZ, xr, zc), BF16),
            vmem((NX, NZ, xr, zc), BF16),
            vmem((NX, NZ, xr, zc), BF16),
            vmem((own_blocks, width, side), BF16),
            vmem((n_tiles, width, side), F32),
            vmem((width, own_rows), F32),
            vmem((NODES, height, side), BF16),
            vmem((NODES, height, side), BF16),
            vmem((10, 1, 128), jnp.int32),
            pltpu.SMEM((10, 1, 128), jnp.int32),
            dma(7), dma(NODES), dma(NODES), dma(3), dma(3), dma(2), dma(2), dma(2), dma(2), dma(3), dma(3),
            dma(3), dma(3), dma(3), dma(3), dma(3), dma(3), dma(4), dma(4), dma(12), dma(12), dma(3), dma(3),
            dma(7), dma(7), dma(7), dma(7), dma(3), dma(3), dma(1), dma(1), dma(NODES), dma(NODES),
        ],
        compiler_params=pltpu.CompilerParams(
            collective_id=0, has_side_effects=True, vmem_limit_bytes=60 << 20
        ),
        name="sage_layer",
    )(row_ids, col_ids, picks, feat, tiles, wn, ws, cot)


def per_device(
    features, tiles, tile_rows, tile_cols, send_rows, send_count, w_neigh, w_self, cotangent
):
    own_rows = features.shape[2]
    parts, slots = send_rows.shape[1:]
    live = lax.broadcasted_iota(jnp.int32, (parts, slots), 1) < send_count[0][:, None]
    picks = jnp.where(live, send_rows[0], -1).reshape(NX, 1, parts * slots // NX)
    grad_scale = float(own_rows * lax.axis_size("node")) ** (-0.5)
    hidden, grad_features, total_neigh, total_self = layer(
        tile_rows, tile_cols, picks, features[0], tiles[0], w_neigh, w_self, cotangent[0], grad_scale
    )
    return hidden[None], grad_features[None], total_neigh, total_self


def solution(mesh):
    placed = (
        P("node", "feat", None),
        P("node", None, None, None),
        P("node", None),
        P("node", None),
        P("node", None, None),
        P("node", None),
        P("feat", None),
        P("feat", None),
        P("node", "feat", None),
    )
    return jax.shard_map(
        per_device,
        mesh=mesh,
        in_specs=placed,
        out_specs=(
            P("node", "feat", None),
            P("node", "feat", None),
            P("feat", None),
            P("feat", None),
        ),
        check_vma=False,
    )
```

time: 129 us -> 120 us (0.930)
  Pallas kernels: 116 us -> 111 us
  local copies, waits for them, and re-layouts: 8.15 us -> 6.75 us
    pallas_call x1, Pallas kernels: 116 us -> 111 us  [layer(): pl.pallas_call(functools.partial(layer_kernel, scale), out_shape=(jax.Sha...]
    squeeze x1 -> x0, local copies, waits for them, and re-layouts: 2.77 us -> none  [per_device(): return (hidden[None], grad_features[None], totals[0], totals[1])]
    unnamed x8 -> x12, local copies, waits for them, and re-layouts: 3.7 us -> 6.34 us
where the time goes in v3:
time: 120 us
  Pallas kernels  111 us (92%)
  local copies, waits for them, and re-layouts  6.75 us (6%)
  other arithmetic  1.93 us (2%)
    pallas_call x1, Pallas kernels, layer(): pl.pallas_call(functools.partial(layer_kernel, scale), out_shape=(jax.Sha...  111 us
    unnamed x12, local copies, waits for them, and re-layouts  6.34 us

profile of v3, /device:TPU:1, one launch (start us, length us, event | category | flops | bytes accessed | tf_op | source)
XLA Modules:
  0.0 120.1 jit_solution(12271284895864241299)
XLA Ops:
  0.6 0.5 broadcast.29
  1.1 1.3 %reduce.3 = s32[64]{0:T(128)S(1)} reduce(s32[1,64]{1,0:T(1,128)} %param.14, s32[]{:T(128)} %broadcast.29), dimensions={0}, to_apply=%param.14.reduce_sub_computation.3 | reduce | bytes 516 | tf_op args[5]
  2.5 0.1 lt.19
  2.5 0.1 iota.12
  2.6 0.1 lt.20
  2.7 0.1 lt.21
  2.8 0.8 copy.14
  3.6 0.1 squeeze.16
  3.7 0.6 compare_select_fusion.picks
  4.3 110.7 %sage_layer.1 = (bf16[512,1024]{1,0:T(8,128)(2,1)}, bf16[192,2048]{1,0:T(8,128)(2,1)}, f32[192,1024]{1,0:T(8,128)}, f32[192,1024]{1,0:T(8,128)}) custom-call(s32[1,48]{1,0:T(1,128)} %row_ref.1, s32[1,48]{1,0:T(1,128)} %col_ref.1, s32[4,1,512]{2,1,0:T(1,128)} %compare_select_fusion.picks, bf16[192,2048]{1,0:T(8,128)(2,1)} %bitcast.8, ...), custom_call_target="tpu_custom_call" | custom-call | tf_op jit(solution)/shard_map/sage_layer/pallas_call | solution.py:435
  115.0 0.0 copy-start.2
  115.1 0.0 copy-start.1
  115.1 2.4 %copy.20 = bf16[1,512,1024]{2,1,0:T(8,128)(2,1)} copy(bf16[1,512,1024]{2,1,0:T(8,128)(2,1)} %bitcast.7) | data formatting | bytes 2097152
  117.4 0.0 copy-done.2
  117.4 0.0 copy-start
  117.5 0.9 copy.21
  118.3 0.0 copy-done.1
  118.3 0.9 copy.22
  119.2 0.0 copy-done
  119.2 0.9 copy.23
  (1 shorter events, 0.0 us)
Async XLA Ops:
  115.0 2.4 %copy-start.2 = (bf16[192,2048]{1,0:T(8,128)(2,1)S(1)}, bf16[192,2048]{1,0:T(8,128)(2,1)}, u32[]{:S(2)}) copy-start(bf16[192,2048]{1,0:T(8,128)(2,1)} %get-tuple-element.9) | copy-start | bytes 2359300
  115.1 3.3 %copy-start.1 = (f32[192,1024]{1,0:T(8,128)S(1)}, f32[192,1024]{1,0:T(8,128)}, u32[]{:S(2)}) copy-start(f32[192,1024]{1,0:T(8,128)} %get-tuple-element.18) | copy-start | bytes 2359300
  117.4 1.8 %copy-start = (f32[192,1024]{1,0:T(8,128)S(1)}, f32[192,1024]{1,0:T(8,128)}, u32[]{:S(2)}) copy-start(f32[192,1024]{1,0:T(8,128)} %get-tuple-element.19) | copy-start | bytes 2359300

commit v4 on v3

--- a/solution.py
+++ b/solution.py
@@ -11,6 +11,8 @@
 NODES = NX * NZ * NC
 GROUP = NZ * NC
 X_ORDER = (2, 1, 3, 0)
+RETURN_ORDER = (0, 2, 1, 3)
+STRIPS = 4
 MESH = pl.DeviceIdType.MESH
 F32 = jnp.float32
 BF16 = jnp.bfloat16
@@ -78,10 +80,11 @@
 
 def layer_kernel(
     scale,
-    row_ref, col_ref, picks, feat_hbm, tiles_hbm, wn_hbm, ws_hbm, cot_hbm,
+    row_ref, col_ref, sends, counts, feat_hbm, tiles_hbm, wn_hbm, ws_hbm, cot_hbm,
     hidden_hbm, gfeat_ref, total_neigh, total_self,
     feat, tiles, cot, weights, onehot, msg_out, msg_in, ext, running, agg_out, cols, pre, gate, hidden,
-    back_out, back_in, own_term, other_term, core_in, x_out, x_in, y_out, y_in, z_out, z_in, z_sum,
+    back_out, back_in, own_term, own_sum, other_term, core_in, x_out, x_in, y_out, y_in,
+    first_y_out, first_y_in, last_x_out, last_x_in, z_out, z_in, z_sum,
     strip, rows, other, blocks, spread, acc,
     ret_out, ret_in, table_rows, table,
     load_sem, halo_send, halo_recv, self_send, self_recv, w_send, w_recv, wf_send, wf_recv, wc_send, wc_recv,
@@ -104,7 +107,8 @@
     side = tiles.shape[1]
     n_tiles = tiles.shape[0]
     own_blocks = own_rows // side
-    lanes = GROUP * 32
+    slots = sends.shape[1]
+    lanes = GROUP * slots
     hid = gate.shape[1]
     xr, zc = width // NX, hid // NZ
     offsets = [(dx, dz, dc) for dx in X_ORDER for dz in range(NZ) for dc in range(NC) if dx or dz or dc]
@@ -143,7 +147,10 @@
 
     def pick(dx):
         part = x_of(dx)
-        wanted = picks[part]
+        near = pl.ds(pl.multiple_of(part * GROUP, GROUP), GROUP)
+        slot = lax.broadcasted_iota(jnp.int32, (GROUP, slots), 1)
+        live = jnp.where(slot < counts[near], sends[near], -1)
+        wanted = jnp.concatenate([live[k:k + 1] for k in range(GROUP)], axis=1)
         ids = lax.broadcasted_iota(jnp.int32, (own_rows, lanes), 0)
         onehot[part] = jnp.where(ids == wanted, 1.0, 0.0).astype(BF16)
         picked = dot(feat[...], onehot[part])
@@ -256,7 +263,7 @@
 
     arrive(selfs)
     arrive(w_core)
-    strips = 4
+    strips = STRIPS
     wide = hid // strips
 
     def self_part(i, carry):
@@ -292,44 +299,124 @@
         backs.append(start(cp))
     back_in[0, y] = dot_last(weights[0, y], gate[...]).astype(BF16)
 
-    y_order = (1, 2, 3, 0)
-    swaps, xs, ys = {}, {}, []
-    for d in y_order:
-        q = y_of(d)
-        other_term[q] = dot(cols[1 - c, q], gate[...]).astype(BF16)
-        swaps[d] = start(remote(other_term.at[q], core_in.at[q], c_send.at[d], c_recv.at[d], partner))
-    for d in y_order:
-        q = y_of(d)
-        term = dot(cols[c, q], gate[...])
-        arrive([swaps[d]])
-        own_term[q] = term + core_in[q].astype(F32)
-        xs[d] = []
-        for e in range(1, NX):
-            at = pl.ds(pl.multiple_of(x_of(e) * xr, xr), xr)
-            x_out[e - 1, q] = own_term[q, at].astype(BF16)
-            k = d * (NX - 1) + e - 1
-            xs[d].append(
-                start(remote(x_out.at[e - 1, q], x_in.at[e - 1, q], x_send.at[k], x_recv.at[k], x_peer(e)))
-            )
-    back_selfs = []
+    swaps, xs, ys = [], [], []
+    for t in range(strips):
+        at = slice(t * wide, (t + 1) * wide)
+        term = dot(cols[1 - c].reshape(NY * width, share), gate[:, at])
+        other_term[t] = term.astype(BF16).reshape(NY, width, wide)
+        swaps.append(start(remote(other_term.at[t], core_in.at[t], c_send.at[t], c_recv.at[t], partner)))
+
+    def sum_over_cores(t):
+        at = slice(t * wide, (t + 1) * wide)
+        term = dot(cols[c].reshape(NY * width, share), gate[:, at]).reshape(NY, width, wide)
+        arrive([swaps[t]])
+        own_term[t] = term + core_in[t].astype(F32)
+
+    my_rows = pl.ds(pl.multiple_of(x * xr, xr), xr)
+    for t in range(strips - 1):
+        sum_over_cores(t)
+        xs.append([])
+        for d in range(1, NX):
+            x_out[t, d - 1] = own_term[t, :, pl.ds(pl.multiple_of(x_of(d) * xr, xr), xr)].astype(BF16)
+            k = t * (NX - 1) + d - 1
+            cp = remote(x_out.at[t, d - 1], x_in.at[t, d - 1], x_send.at[k], x_recv.at[k], x_peer(d))
+            xs[t].append(start(cp))
+    sum_over_cores(strips - 1)
+    first_ys = []
     for d in range(1, NY):
-        q = y_of(d)
-        back_out[1, q] = dot_last(weights[1, q], gate[...]).astype(BF16)
-        cp = remote(back_out.at[1, q], back_in.at[1, y], bs_send.at[d - 1], bs_recv.at[d - 1], y_peer(d))
-        back_selfs.append(start(cp))
+        first_y_out[d - 1] = own_term[strips - 1, y_of(d)].astype(BF16)
+        k = (strips - 1) * (NY - 1) + d - 1
+        cp = remote(first_y_out.at[d - 1], first_y_in.at[d - 1], y_send.at[k], y_recv.at[k], y_peer(d))
+        first_ys.append(start(cp))
+
+    def x_to_y(t):
+        arrive(xs[t])
+        mine = own_term[t, :, my_rows]
+        for d in range(1, NX):
+            mine = mine + x_in[t, d - 1].astype(F32)
+        own_sum[t] = mine
+        ys.append([])
+        for d in range(1, NY):
+            y_out[t, d - 1] = own_sum[t, y_of(d)].astype(BF16)
+            k = t * (NY - 1) + d - 1
+            cp = remote(y_out.at[t, d - 1], y_in.at[t, d - 1], y_send.at[k], y_recv.at[k], y_peer(d))
+            ys[t].append(start(cp))
+
+    last_xs, xgs = [], []
+
+    def y_to_x():
+        arrive(first_ys)
+        mine = own_term[strips - 1, y]
+        for d in range(1, NY):
+            mine = mine + first_y_in[d - 1].astype(F32)
+        own_term[strips - 1, y] = mine
+        for d in range(1, NX):
+            rows_of = pl.ds(pl.multiple_of(x_of(d) * xr, xr), xr)
+            last_x_out[d - 1] = own_term[strips - 1, y, rows_of].astype(BF16)
+            k = (strips - 1) * (NX - 1) + d - 1
+            cp = remote(last_x_out.at[d - 1], last_x_in.at[d - 1], x_send.at[k], x_recv.at[k], x_peer(d))
+            last_xs.append(start(cp))
+
+    for d in range(1, NY):
+        back_out[1, y_of(d)] = dot_last(weights[1, y_of(d)], gate[...]).astype(BF16)
     back_in[1, y] = dot_last(weights[1, y], gate[...]).astype(BF16)
 
-    def sum_over_x(d):
-        q = y_of(d)
-        arrive(xs[d])
-        mine = own_term[q, pl.ds(pl.multiple_of(x * xr, xr), xr)]
-        for e in range(1, NX):
-            mine = mine + x_in[e - 1, q].astype(F32)
-        return mine
-
-    def send_over_y(d):
-        y_out[d - 1] = sum_over_x(d).astype(BF16)
-        ys.append(start(remote(y_out.at[d - 1], y_in.at[d - 1], y_send.at[d - 1], y_recv.at[d - 1], y_peer(d))))
+    per_strip = wide // zc
+    maybe_started, lasts = [], []
+
+    def sum_over_y(t):
+        if t < strips - 1:
+            arrive(ys[t])
+            mine = own_sum[t, y]
+            for d in range(1, NY):
+                mine = mine + y_in[t, d - 1].astype(F32)
+        else:
+            arrive(last_xs)
+            mine = own_term[t, y, my_rows]
+            for d in range(1, NX):
+                mine = mine + last_x_in[d - 1].astype(F32)
+        for u in range(per_strip):
+            piece = t * per_strip + u
+            z_out[piece] = mine[:, u * zc:(u + 1) * zc].astype(BF16)
+            k = lax.rem(piece - z + NZ - 1, NZ)
+            cp = remote(z_out.at[piece], z_in.at[k], z_send.at[k], z_recv.at[k], {"node": node_of(x, piece, c)})
+            pl.when(z != piece)(cp.start)
+            maybe_started.append((z != piece, cp))
+
+    def piece_copy(d):
+        return remote(z_sum, strip.at[z], zg_send.at[d - 1], zg_recv.at[d - 1], z_peer(d))
+
+    def sum_over_z(t):
+        @pl.when(lax.div(z, per_strip) == t)
+        def _():
+            mine = z_out[z].astype(F32)
+            for d in range(1, NZ):
+                remote(z_out.at[z], z_in.at[d - 1], z_send.at[d - 1], z_recv.at[d - 1], z_peer(d)).wait_recv()
+                mine = mine + z_in[d - 1].astype(F32)
+            z_sum[...] = mine.astype(BF16)
+            for d in range(1, NZ):
+                piece_copy(d).start()
+            strip[z] = z_sum[...]
+
+    def gather_over_x(t):
+        for u in range(per_strip):
+            piece = t * per_strip + u
+            k = lax.rem(z - piece + NZ - 1, NZ)
+            cp = remote(z_sum, strip.at[piece], zg_send.at[k], zg_recv.at[k], {"node": node_of(x, piece, c)})
+            pl.when(z != piece)(cp.wait_recv)
+        pieces = pl.ds(t * per_strip, per_strip)
+        xgs.append([])
+        for d in range(1, NX):
+            k = t * (NX - 1) + d - 1
+            cp = remote(strip.at[pieces], rows.at[x, pieces], xg_send.at[k], xg_recv.at[k], x_peer(d))
+            xgs[t].append(start(cp))
+        rows[x, pieces] = strip[pieces]
+
+    def gather_over_cores(t):
+        arrive(xgs[t])
+        pieces = pl.ds(t * per_strip, per_strip)
+        cp = remote(rows.at[:, pieces], other.at[:, pieces], cg_send.at[t], cg_recv.at[t], partner)
+        lasts.append(start(cp))
 
     arrive(backs)
     for r in range(own_blocks):
@@ -363,52 +450,47 @@
         acc[...] += dot_last(came, onehot[part])
 
     ret_in[n] = jnp.zeros(ret_in.shape[1:], BF16)
-    send_back(X_ORDER[0])
-    send_over_y(1)
-    send_over_y(2)
-    send_back(X_ORDER[1])
-    send_over_y(3)
-    mine = sum_over_x(0)
-    arrive(ys)
+    x_to_y(0)
+    send_back(RETURN_ORDER[0])
+    send_back(RETURN_ORDER[1])
+    send_back(RETURN_ORDER[2])
+    send_back(RETURN_ORDER[3])
+    for b in range(own_blocks):
+        acc[:, b * side:(b + 1) * side] = spread[table[8, 0, b]] * table[9, 0, b].astype(F32)
+    x_to_y(1)
+    sum_over_y(0)
+    x_to_y(2)
+    y_to_x()
+    sum_over_y(1)
+    sum_over_y(2)
+    sum_over_y(3)
+    back_selfs = []
     for d in range(1, NY):
-        mine = mine + y_in[d - 1].astype(F32)
-    for q in range(NZ):
-        z_out[q] = mine[:, q * zc:(q + 1) * zc].astype(BF16)
-    zs = []
-    for d in range(1, NZ):
-        cp = remote(z_out.at[z_of(d)], z_in.at[d - 1], z_send.at[d - 1], z_recv.at[d - 1], z_peer(d))
-        zs.append(start(cp))
-    send_back(X_ORDER[2])
+        cp = remote(
+            back_out.at[1, y_of(d)], back_in.at[1, y], bs_send.at[d - 1], bs_recv.at[d - 1], y_peer(d)
+        )
+        back_selfs.append(start(cp))
+    sum_over_z(0)
+    sum_over_z(1)
+    sum_over_z(2)
+    sum_over_z(3)
+    gather_over_x(0)
+    gather_over_x(1)
+    gather_over_x(2)
+    gather_over_x(3)
+    scatter(RETURN_ORDER[0])
+    gather_over_cores(0)
+    gather_over_cores(1)
+    gather_over_cores(2)
+    gather_over_cores(3)
+    scatter(RETURN_ORDER[1])
+    scatter(RETURN_ORDER[2])
+    scatter(RETURN_ORDER[3])
     arrive(back_selfs)
-    for b in range(own_blocks):
-        at = slice(b * side, (b + 1) * side)
-        inner = slice((b % per) * side, (b % per + 1) * side)
-        acc[:, at] = spread[table[8, 0, b]] * table[9, 0, b].astype(F32) + back_in[1, b // per, :, inner].astype(F32)
-    arrive(zs)
-    mine = z_out[z].astype(F32)
-    for d in range(1, NZ):
-        mine = mine + z_in[d - 1].astype(F32)
-    z_sum[...] = mine.astype(BF16)
-    zgs = []
-    for d in range(1, NZ):
-        cp = remote(z_sum, strip.at[z], zg_send.at[d - 1], zg_recv.at[d - 1], z_peer(d))
-        zgs.append(start(cp))
-    strip[z] = z_sum[...]
-    send_back(X_ORDER[3])
-    scatter(X_ORDER[0])
-    arrive(zgs)
-    xgs = []
-    for d in range(1, NX):
-        cp = remote(strip, rows.at[x], xg_send.at[d - 1], xg_recv.at[d - 1], x_peer(d))
-        xgs.append(start(cp))
-    rows[x] = strip[...]
-    scatter(X_ORDER[1])
-    arrive(xgs)
-    last = start(remote(rows, other, cg_send.at[0], cg_recv.at[0], partner))
-    for dx in X_ORDER[2:]:
-        scatter(dx)
-    gfeat_ref[...] = acc[...].astype(BF16)
-    arrive([last])
+    for q in range(NY):
+        at = slice(q * share, (q + 1) * share)
+        gfeat_ref[:, at] = (acc[:, at] + back_in[1, q].astype(F32)).astype(BF16)
+    arrive(lasts)
     for a in range(NX):
         for b in range(NZ):
             ra, cb = slice(a * xr, (a + 1) * xr), slice(b * zc, (b + 1) * zc)
@@ -418,9 +500,13 @@
     store_hidden.wait()
     for cp in started:
         cp.wait_send()
-
-
-def layer(row_ids, col_ids, picks, feat, tiles, wn, ws, cot, scale):
+    for condition, cp in maybe_started:
+        pl.when(condition)(cp.wait_send)
+    for d in range(1, NZ):
+        piece_copy(d).wait_send()
+
+
+def layer(row_ids, col_ids, sends, counts, feat, tiles, wn, ws, cot, scale):
     width, own_rows = feat.shape
     n_tiles, side, _ = tiles.shape
     share, hid = cot.shape
@@ -428,6 +514,7 @@
     own_blocks = own_rows // side
     lanes = own_rows // NX
     height = width // 4
+    strips, wide = STRIPS, hid // STRIPS
     vmem = pltpu.VMEM
     dma = lambda k: pltpu.SemaphoreType.DMA((k,))
     any_space = pl.BlockSpec(memory_space=pl.ANY)
@@ -440,7 +527,7 @@
             jax.ShapeDtypeStruct((width, hid), F32),
             jax.ShapeDtypeStruct((width, hid), F32),
         ),
-        in_specs=[in_vmem] * 3 + [any_space] * 5,
+        in_specs=[in_vmem] * 4 + [any_space] * 5,
         out_specs=(any_space, in_vmem, in_vmem, in_vmem),
         scratch_shapes=[
             vmem((width, own_rows), BF16),
@@ -459,15 +546,20 @@
             vmem((share, hid), BF16),
             vmem((2, NY, width, share), BF16),
             vmem((2, NY, width, share), BF16),
-            vmem((NY, width, hid), F32),
-            vmem((NY, width, hid), BF16),
-            vmem((NY, width, hid), BF16),
-            vmem((NX - 1, NY, xr, hid), BF16),
-            vmem((NX - 1, NY, xr, hid), BF16),
-            vmem((NY - 1, xr, hid), BF16),
-            vmem((NY - 1, xr, hid), BF16),
+            vmem((strips, NY, width, wide), F32),
+            vmem((strips - 1, NY, xr, wide), F32),
+            vmem((strips, NY, width, wide), BF16),
+            vmem((strips, NY, width, wide), BF16),
+            vmem((strips - 1, NX - 1, NY, xr, wide), BF16),
+            vmem((strips - 1, NX - 1, NY, xr, wide), BF16),
+            vmem((strips - 1, NY - 1, xr, wide), BF16),
+            vmem((strips - 1, NY - 1, xr, wide), BF16),
+            vmem((NY - 1, width, wide), BF16),
+            vmem((NY - 1, width, wide), BF16),
+            vmem((NX - 1, xr, wide), BF16),
+            vmem((NX - 1, xr, wide), BF16),
             vmem((NZ, xr, zc), BF16),
-            vmem((NZ - 1, xr, zc), BF16),
+            vmem((NZ, xr, zc), BF16),
             vmem((xr, zc), BF16),
             vmem((NZ, xr, zc), BF16),
             vmem((NX, NZ, xr, zc), BF16),
@@ -480,27 +572,52 @@
             vmem((10, 1, 128), jnp.int32),
             pltpu.SMEM((10, 1, 128), jnp.int32),
             dma(7), dma(NODES), dma(NODES), dma(3), dma(3), dma(2), dma(2), dma(2), dma(2), dma(3), dma(3),
-            dma(3), dma(3), dma(3), dma(3), dma(3), dma(3), dma(4), dma(4), dma(12), dma(12), dma(3), dma(3),
-            dma(7), dma(7), dma(7), dma(7), dma(3), dma(3), dma(1), dma(1), dma(NODES), dma(NODES),
+            dma(3), dma(3), dma(3), dma(3), dma(3), dma(3), dma(4), dma(4), dma(12), dma(12), dma(12), dma(12),
+            dma(8), dma(8), dma(8), dma(8), dma(12), dma(12), dma(4), dma(4), dma(NODES), dma(NODES),
         ],
         compiler_params=pltpu.CompilerParams(
             collective_id=0, has_side_effects=True, vmem_limit_bytes=60 << 20
         ),
         name="sage_layer",
-    )(row_ids, col_ids, picks, feat, tiles, wn, ws, cot)
+    )(row_ids, col_ids, sends, counts, feat, tiles, wn, ws, cot)
+
+
+def settle_kernel(*refs):
+    count = (len(refs) - 1) // 3
+    sources, targets, held, sems = refs[:count], refs[count:2 * count], refs[2 * count:-1], refs[-1]
+    taken = [pltpu.make_async_copy(sources[i], held[i], sems.at[0, i]) for i in range(count)]
+    put = [pltpu.make_async_copy(held[i], targets[i], sems.at[1, i]) for i in range(count)]
+    for cp in taken:
+        cp.start()
+    for i in range(count):
+        taken[i].wait()
+        put[i].start()
+    for cp in put:
+        cp.wait()
+
+
+def settle(arrays):
+    spec = pl.BlockSpec(memory_space=pl.ANY)
+    return pl.pallas_call(
+        settle_kernel,
+        out_shape=tuple(jax.ShapeDtypeStruct(a.shape, a.dtype) for a in arrays),
+        in_specs=[spec] * len(arrays),
+        out_specs=(spec,) * len(arrays),
+        scratch_shapes=[pltpu.VMEM(a.shape, a.dtype) for a in arrays]
+        + [pltpu.SemaphoreType.DMA((2, len(arrays)))],
+        name="settle",
+    )(*arrays)
 
 
 def per_device(
     features, tiles, tile_rows, tile_cols, send_rows, send_count, w_neigh, w_self, cotangent
 ):
     own_rows = features.shape[2]
-    parts, slots = send_rows.shape[1:]
-    live = lax.broadcasted_iota(jnp.int32, (parts, slots), 1) < send_count[0][:, None]
-    picks = jnp.where(live, send_rows[0], -1).reshape(NX, 1, parts * slots // NX)
     grad_scale = float(own_rows * lax.axis_size("node")) ** (-0.5)
-    hidden, grad_features, total_neigh, total_self = layer(
-        tile_rows, tile_cols, picks, features[0], tiles[0], w_neigh, w_self, cotangent[0], grad_scale
+    results = layer(
+        tile_rows, tile_cols, send_rows[0], send_count.reshape(-1, 1), features[0], tiles[0], w_neigh, w_self, cotangent[0], grad_scale
     )
+    hidden, grad_features, total_neigh, total_self = settle(results)
     return hidden[None], grad_features[None], total_neigh, total_self
 
 

time: 120 us -> 114 us (0.950)
  local copies, waits for them, and re-layouts: 6.75 us -> 2.77 us
  Pallas kernels: 111 us -> 109 us
  other arithmetic: 1.93 us -> 0 us
    unnamed x12 -> x1, local copies, waits for them, and re-layouts: 6.34 us -> 1.42 us
    pallas_call x1, Pallas kernels: 111 us -> 106 us  [layer(): pl.pallas_call(functools.partial(layer_kernel, scale), out_shape=(jax.Sha...]
    pallas_call x0 -> x1, Pallas kernels: none -> 3.04 us  [settle(): pl.pallas_call(settle_kernel, out_shape=tuple((jax.ShapeDtypeStruct(a.sha...]
    reshape x0 -> x1, local copies, waits for them, and re-layouts: none -> 1.36 us  [per_device(): send_count.reshape(-1, 1)]
    unnamed x1 -> x0, other arithmetic: 1.32 us -> none
where the time goes in v4:
time: 114 us; the launch traced here: 113 us
  Pallas kernels  109 us (96%)
  local copies, waits for them, and re-layouts  2.77 us (2%)
    pallas_call x1, Pallas kernels, layer(): pl.pallas_call(functools.partial(layer_kernel, scale), out_shape=(jax.Sha...  106 us
    pallas_call x1, Pallas kernels, settle(): pl.pallas_call(settle_kernel, out_shape=tuple((jax.ShapeDtypeStruct(a.sha...  3.04 us

profile of v4, /device:TPU:1, one launch (start us, length us, event | category | flops | bytes accessed | tf_op | source)
XLA Modules:
  0.0 112.9 jit_solution(15727712876011216315)
XLA Ops:
  0.6 1.4 %copy.13 = s32[1,64,32]{2,1,0:T(8,128)} copy(s32[1,64,32]{1,2,0:T(8,128)} %param.13) | data formatting | bytes 16384 | tf_op args[4]
  2.0 1.4 %copy.14.counts = s32[64,1]{1,0:T(8,128)} copy(s32[64,1]{0,1:T(1,128)} %bitcast.11) | data formatting | bytes 512 | tf_op jit(solution)/shard_map/reshape | solution.py:618
  3.4 106.3 %sage_layer.1 = (bf16[512,1024]{1,0:T(8,128)(2,1)}, bf16[192,2048]{1,0:T(8,128)(2,1)}, f32[192,1024]{1,0:T(8,128)}, f32[192,1024]{1,0:T(8,128)}) custom-call(s32[1,48]{1,0:T(1,128)} %row_ref.1, s32[1,48]{1,0:T(1,128)} %col_ref.1, s32[64,32]{1,0:T(8,128)} %bitcast.10, s32[64,1]{1,0:T(8,128)} %copy.14.counts, bf16[192,2048]{1,0:T(8,128)(2,1)} %bitcast.9, ...), custom_call_target="tpu_custom_call" | custom-call | tf_op jit(solution)/shard_map/sage_layer/pallas_call | solution.py:522
  109.7 3.0 %settle.1 = (bf16[512,1024]{1,0:T(8,128)(2,1)}, bf16[192,2048]{1,0:T(8,128)(2,1)}, f32[192,1024]{1,0:T(8,128)}, f32[192,1024]{1,0:T(8,128)}) custom-call(bf16[512,1024]{1,0:T(8,128)(2,1)} %get-tuple-element.12.refs_0_, bf16[192,2048]{1,0:T(8,128)(2,1)} %get-tuple-element.13.refs_1_, f32[192,1024]{1,0:T(8,128)} %get-tuple-element.14.refs_2_, ...), custom_call_target="tpu_custom_call" | custom-call | tf_op jit(solution)/shard_map/settle/pallas_call | solution.py:601
